TPU v7x, 256 devices: a whole 4x4x8 slice. The times are simulated.
256 devices in a mesh: layer: 16 (over x_lo, z), tok: 16 (over y, x_hi, core).
Axes of the slice: x: 4 (x_hi: 2, x_lo: 2; x = x_hi * 2 + x_lo), y: 4, z: 8, core: 2. Of those that a mesh axis runs over, the one named last changes fastest.
Arguments:
- acts: bfloat16 [16, 512, 2048], P('layer', 'tok'), may hold values from -6 to 6
- w_enc: bfloat16 [16, 2048, 1024], P('layer', 'tok'), may hold values from -0.125 to 0.125
- b_enc: float32 [16, 1024], P('layer'), may hold values from -0.5 to 0.5
- w_dec: bfloat16 [16, 16, 1024, 2048], P('layer', None, None, 'tok'), may hold values from -0.046875 to 0.046875
- targets: bfloat16 [16, 512, 2048], P('layer', None, 'tok'), may hold values from -6 to 6
Outputs:
- code_grad: float32 [16, 512, 1024], P('layer', 'tok')
- dec_grad: bfloat16 [16, 16, 1024, 2048], P('layer', None, None, 'tok')
All inputs are finite; a program needn't handle non-finite values.
Results may differ from a plain program's by a relative error of at most 0.0034.
Values may be sent and summed in bfloat16 or wider, within the bound.
No kernel may reach another device: no remote copies, remote signals or barrier semaphores. Data moves between devices by JAX's collectives and lax.ppermute only.
A program may use at most 64 MiB of HBM per device.

v0:
```python
import jax
import jax.numpy as jnp
from jax import lax
from jax.sharding import PartitionSpec as P


def project(lower, upper, source, dec_slabs, offset, partials):

    def project_advance(index, total):
        weight_slab = lax.dynamic_index_in_dim(dec_slabs, index, 0, keepdims=False)
        product = jnp.dot(source, weight_slab, preferred_element_type=jnp.float32)
        current = lax.dynamic_index_in_dim(total, index + offset, 0, keepdims=True)
        return lax.dynamic_update_index_in_dim(total, current + product[None], index + offset, 0)

    return lax.fori_loop(lower, upper, project_advance, partials)


def backprop(lower, upper, source, dec_slabs, offset, errors):
    features = source.shape[1]
    source_wide = source.astype(jnp.float32)
    empty_grads = jnp.zeros(dec_slabs.shape, jnp.bfloat16)
    empty_codes = jnp.zeros((source.shape[0], features), jnp.float32)

    def backprop_advance(index, carry):
        weight_grads, code_partial = carry
        weight_slab = lax.dynamic_index_in_dim(dec_slabs, index, 0, keepdims=False).astype(
            jnp.float32
        )
        error_block = lax.dynamic_index_in_dim(errors, index + offset, 0, keepdims=False)
        block_grad = lax.dot_general(
            source_wide,
            error_block,
            (((0,), (0,)), ((), ())),
            precision=lax.Precision.HIGHEST,
            preferred_element_type=jnp.float32,
        )
        weight_grads = lax.dynamic_update_index_in_dim(
            weight_grads, block_grad.astype(jnp.bfloat16)[None], index, 0
        )
        code_partial = code_partial + lax.dot_general(
            error_block,
            weight_slab,
            (((1,), (1,)), ((), ())),
            precision=lax.Precision.HIGHEST,
            preferred_element_type=jnp.float32,
        )
        return (weight_grads, code_partial)

    return lax.fori_loop(lower, upper, backprop_advance, (empty_grads, empty_codes))


def local(acts, w_enc, b_enc, w_dec, targets):
    layers = lax.axis_size("layer")
    layer_index = lax.axis_index("layer")
    own_acts = acts[0]
    columns = own_acts
    preact = jnp.dot(
        columns,
        lax.all_gather(w_enc, "tok", axis=1, tiled=True)[0],
        preferred_element_type=jnp.float32,
    )
    own_codes = jnp.maximum(preact + b_enc, 0.0).astype(jnp.bfloat16)
    feature_codes = lax.all_gather(own_codes, "tok", axis=0, tiled=True)
    dec_slabs = w_dec[0]
    tokens = feature_codes.shape[0]
    columns = dec_slabs.shape[2]
    partials = jnp.zeros((layers, tokens, columns), jnp.float32)
    partials = project(layer_index, layers, feature_codes, dec_slabs, 0, partials)
    own_targets = targets[0].astype(jnp.float32)
    current = lax.dynamic_index_in_dim(partials, layer_index, 0, keepdims=True)
    partials = lax.dynamic_update_index_in_dim(
        partials, current - own_targets[None], layer_index, 0
    )
    errors = lax.psum(partials, "layer")
    weight_grads, code_partial = backprop(layer_index, layers, feature_codes, dec_slabs, 0, errors)
    code_share = lax.psum_scatter(code_partial, "tok", scatter_dimension=0, tiled=True)
    return (code_share[None], weight_grads[None])


def solution(mesh):
    return jax.shard_map(
        local,
        mesh=mesh,
        in_specs=(
            P("layer", "tok", None),
            P("layer", "tok", None),
            P("layer", None),
            P("layer", None, None, "tok"),
            P("layer", None, "tok"),
        ),
        out_specs=(P("layer", "tok", None), P("layer", None, None, "tok")),
        check_vma=False,
    )
```

profile of v0, /device:TPU:32, one launch (start us, length us, event | category | flops | bytes accessed | tf_op | source)
XLA Modules:
  0.0 520.1 jit_solution(11160938395060263424)
XLA Ops:
  8.0 65.3 %all-gather.3.cloned.1.call-done = bf16[1,2048,1024]{2,1,0:T(8,128)(2,1)} async-done(((bf16[1,128,1024]{2,1,0:T(8,128)(2,1)}), bf16[1,2048,1024]{2,1,0:T(8,128)(2,1)}) %all-gather.3.cloned.1.call-update) | async-done | bytes 4194320 | tf_op jit(solution)/shard_map/all_gather | solution.py:59
  73.2 3.7 fusion.21
  77.0 47.8 %all-gather.5.cloned.1.call-done = bf16[512,1024]{1,0:T(8,128)(2,1)} async-done(((bf16[32,1024]{1,0:T(8,128)(2,1)}), bf16[512,1024]{1,0:T(8,128)(2,1)}) %all-gather.5.cloned.1.call-update) | async-done | bytes 1048592 | tf_op jit(solution)/shard_map/all_gather | solution.py:63
  124.7 2.5 broadcast_in_dim.24.clone
  127.2 51.2 %while.22 = (s32[]{:T(128)}, f32[16,512,128]{2,1,0:T(8,128)}, bf16[16,1024,128]{2,1,0:T(8,128)(2,1)}, bf16[512,1024]{1,0:T(8,128)(2,1)S(1)}, s32[]{:T(128)}, /*index=5*/s32[]{:T(128)}, s32[]{:T(128)}) while((s32[]{:T(128)}, f32[16,512,128]{2,1,0:T(8,128)}, bf16[16,1024,128]{2,1,0:T(8,128)(2,1)}, bf16[512,1024]{1,0:T(8,128)(2,1)S(1)}, ...), condition=%wide.region_1.2_spmd, body=%wide.region_0.1_spmd.sunk | while | flops 134283264 | bytes 3932291 | solution.py:15
  127.2 1.0 constant_dynamic-slice_fusion.2
  128.3 1.4 fusion.37
  130.6 1.0 constant_dynamic-slice_fusion.2
  131.8 1.4 fusion.37
  134.1 1.0 constant_dynamic-slice_fusion.2
  135.2 1.4 fusion.37
  137.5 1.0 constant_dynamic-slice_fusion.2
  138.6 1.4 fusion.37
  140.9 1.0 constant_dynamic-slice_fusion.2
  142.0 1.4 fusion.37
  144.3 1.0 constant_dynamic-slice_fusion.2
  145.4 1.4 fusion.37
  147.7 1.0 constant_dynamic-slice_fusion.2
  148.8 1.4 fusion.37
  152.2 1.4 fusion.37
  155.6 1.4 fusion.37
  159.0 1.4 fusion.37
  162.4 1.4 fusion.37
  165.8 1.4 fusion.37
  169.2 1.4 fusion.37
  172.7 1.4 fusion.37
  176.1 1.4 fusion.37
  178.4 1.7 subtract_dynamic-update-slice_fusion
  180.1 1.6 convert_element_type.19
  181.7 147.9 %all-reduce.2.cloned.1.call-done = f32[16,512,128]{2,1,0:T(8,128)} async-done(((f32[16,512,128]{2,1,0:T(8,128)}), f32[16,512,128]{2,1,0:T(8,128)}) %all-reduce.2.cloned.1.call-update) | async-done | bytes 4194320 | tf_op jit(solution)/shard_map/psum | solution.py:74
  329.8 2.8 broadcast_in_dim.22.clone
  332.7 96.6 %while.23 = (s32[]{:T(128)}, bf16[16,1024,128]{2,1,0:T(8,128)(2,1)}, f32[512,1024]{1,0:T(8,128)S(1)}, f32[16,512,128]{2,1,0:T(8,128)}, f32[512,1024]{1,0:T(8,128...) while((s32[]{:T(128)}, bf16[16,1024,128]{2,1,0:T(8,128)(2,1)}, ...), condition=%wide.region_4.5_spmd, body=%wide.region_3.4_spmd.sunk | while | flops 1611268096 | bytes 8389775 | solution.py:49
  332.7 3.0 fusion.42
  335.8 2.6 convolution_add_fusion.2
  339.1 3.0 fusion.42
  342.2 2.6 convolution_add_fusion.2
  345.5 3.0 fusion.42
  348.7 2.6 convolution_add_fusion.2
  352.0 3.0 fusion.42
  355.1 2.6 convolution_add_fusion.2
  358.4 3.0 fusion.42
  361.6 2.6 convolution_add_fusion.2
  364.9 3.0 fusion.42
  368.0 2.6 convolution_add_fusion.2
  371.3 3.0 fusion.42
  374.4 2.6 convolution_add_fusion.2
  377.7 3.0 fusion.42
  380.9 2.6 convolution_add_fusion.2
  384.2 3.0 fusion.42
  387.3 2.6 convolution_add_fusion.2
  390.6 3.0 fusion.42
  393.8 2.6 convolution_add_fusion.2
  397.1 3.0 fusion.42
  400.2 2.6 convolution_add_fusion.2
  403.5 3.0 fusion.42
  406.7 2.6 convolution_add_fusion.2
  410.0 3.0 fusion.42
  413.1 2.6 convolution_add_fusion.2
  416.4 3.0 fusion.42
  419.5 2.6 convolution_add_fusion.2
  422.8 3.0 fusion.42
  426.0 2.6 convolution_add_fusion.2
  429.3 1.3 copy-done.1
  430.6 82.9 %reduce-scatter.2.cloned.1.call-done = f32[32,1024]{1,0:T(8,128)} async-done(((f32[512,1024]{1,0:T(8,128)}), f32[32,1024]{1,0:T(8,128)}) %reduce-scatter.2.cloned.1.call-update) | async-done | bytes 131088 | tf_op jit(solution)/shard_map/reduce_scatter | solution.py:76
  (99 shorter events, 36.9 us)
Async XLA Ops:
  7.2 66.1 %copy-start = (bf16[1,32,2048]{2,1,0:T(8,128)(2,1)S(1)}, bf16[1,32,2048]{2,1,0:T(8,128)(2,1)}, u32[]{:S(2)}) copy-start(bf16[1,32,2048]{2,1,0:T(8,128)(2,1)} %param.9) | copy-start | bytes 393220
  7.2 66.1 %all-gather.3.cloned.1.call-start = ((), (), s32[]{:S(2)}) async-start(), calls=%async_computation.1 | async-start | bytes 4456448 | tf_op jit(solution)/shard_map/all_gather | solution.py:59
  7.9 116.8 %all-gather.5.cloned.1.call-start = ((), (), s32[]{:S(2)}) async-start(), calls=%async_computation.2 | async-start | bytes 1114112 | tf_op jit(solution)/shard_map/all_gather | solution.py:63
  76.9 252.7 %all-reduce.2.cloned.1.call-start = ((), (), s32[]{:S(2)}) async-start(), calls=%async_computation.3 | async-start | bytes 8388608 | tf_op jit(solution)/shard_map/psum | solution.py:74
  124.7 2.5 copy-start.2
  127.2 51.2 %copy-start.3 = (bf16[1,512,128]{2,1,0:T(8,128)(2,1)S(1)}, bf16[1,512,128]{2,1,0:T(8,128)(2,1)}, u32[]{:S(2)}) copy-start(bf16[1,512,128]{2,1,0:T(8,128)(2,1)} %param.13) | copy-start | bytes 393220
  180.1 333.5 %reduce-scatter.2.cloned.1.call-start = ((), (), s32[]{:S(2)}) async-start(), calls=%async_computation.4 | async-start | bytes 2228224 | tf_op jit(solution)/shard_map/reduce_scatter | solution.py:76
  429.3 1.3 copy-start.1
Sparse Core Ops, SparseCore 0:
  10.7 62.4 all-gather.2
  77.0 47.6 all-gather.4
  180.2 149.3 all-reduce.1
  430.8 82.7 reduce-scatter.1
where the time goes:
time: 522 us; the launch traced here: 520 us
  waiting for transfers between devices  345 us (66%)
  matrix products  108 us (21%)
  local copies, waits for them, and re-layouts  49.5 us (9%)
  between operations  13.8 us (3%)
    psum x1, waiting for transfers between devices, local(): errors = lax.psum(partials, 'layer')  148 us
    reduce_scatter x1, waiting for transfers between devices, local(): lax.psum_scatter(code_partial, 'tok', scatter_dimension=0, tiled=True)  82.9 us
    all_gather x1, waiting for transfers between devices, local(): lax.all_gather(w_enc, 'tok', axis=1, tiled=True)[0]  65.3 us
    all_gather x1, waiting for transfers between devices, local(): feature_codes = lax.all_gather(own_codes, 'tok', axis=0, tiled=True)  47.8 us
    dot_general x15, matrix products, backprop_advance(): lax.dot_general(source_wide, error_block, (((0,), (0,)), ((), ())), preci...  44.5 us
    dot_general x15, matrix products, backprop_advance(): lax.dot_general(error_block, weight_slab, (((1,), (1,)), ((), ())), preci...  38.4 us
    dot_general x15, matrix products, project_advance(): product = jnp.dot(source, weight_slab, preferred_element_type=jnp.float32)  21.6 us
    dynamic_slice x30, local copies, waits for them, and re-layouts, project_advance(): current = lax.dynamic_index_in_dim(total, index + offset, 0, keepdims=True)  16.5 us
  transfers between devices with their start and end apart: 4, of which 4 were waited for; matrix products, arithmetic and copies ran while one was open for 0% of the time, Pallas kernels for 0%

commit v1 on v0

v1 whole, which is shorter than its diff:
```python
import functools

import jax
import jax.numpy as jnp
from jax import lax
from jax.experimental import pallas as pl
from jax.experimental.pallas import tpu as pltpu
from jax.sharding import PartitionSpec as P

BF = jnp.bfloat16
F32 = jnp.float32
AXES = ("layer", "tok")
NL, NT, NZ = 16, 16, 8


def _layer_perm(fn):
    return [(l * NT + t, fn(l) * NT + t) for l in range(NL) for t in range(NT)]


def _tok_perm(fn):
    return [(l * NT + t, l * NT + fn(t)) for l in range(NL) for t in range(NT)]


Z_UP = _layer_perm(lambda l: (l // NZ) * NZ + (l + 1) % NZ)
Z_DOWN = _layer_perm(lambda l: (l // NZ) * NZ + (l - 1) % NZ)
X_SWAP = _layer_perm(lambda l: l ^ NZ)
CORE_SWAP = _tok_perm(lambda t: t ^ 1)
XHI_SWAP = _tok_perm(lambda t: t ^ 2)

G_PLANE = [[y * 4 + q for q in range(4)] for y in range(4)]
G_Y = [[y * 4 + q for y in range(4)] for q in range(4)]
G_CHIP = [[y * 4 + xh * 2 + c for xh in range(2) for y in range(4)] for c in range(2)]


def permute(x, pairs):
    return lax.ppermute(x, AXES, pairs)


def swap_blocks(x, groups):
    return lax.all_to_all(x, "tok", 0, 0, axis_index_groups=groups)


def spread(x, groups):
    return swap_blocks(jnp.broadcast_to(x[None], (len(groups[0]),) + x.shape), groups)


def call(kernel, grid, in_specs, out_specs, out_shape, scratch, flops, nbytes, aliases=None):
    return pl.pallas_call(
        kernel,
        grid_spec=pltpu.PrefetchScalarGridSpec(
            num_scalar_prefetch=1,
            grid=grid,
            in_specs=in_specs,
            out_specs=out_specs,
            scratch_shapes=scratch,
        ),
        out_shape=out_shape,
        input_output_aliases=aliases or {},
        cost_estimate=pl.CostEstimate(flops=flops, bytes_accessed=nbytes, transcendentals=0),
        compiler_params=pltpu.CompilerParams(vmem_limit_bytes=40 << 20),
    )


def whole(shape):
    return pl.BlockSpec(shape, lambda *_: (0,) * len(shape))


def encode_kernel(pos, a0, a1, a2, w_ref, b_ref, out_ref, acts):
    q = pos[2]
    for r, part in enumerate((a0, a1, a2.at[0], a2.at[1])):
        acts[pl.ds(pl.multiple_of((q ^ r) * 32, 32), 32), :] = part[...]
    pre = jnp.dot(acts[...], w_ref[...], preferred_element_type=F32)
    out_ref[...] = jnp.maximum(pre + b_ref[...], 0.0).astype(BF)


def encode(pos, a0, a1, a2, w, b):
    return call(
        encode_kernel,
        (1,),
        [
            whole(a0.shape),
            whole(a1.shape),
            whole(a2.shape),
            whole(w.shape),
            pl.BlockSpec((1, 256), lambda i, pos: (0, pos[2])),
        ],
        whole((128, 256)),
        jax.ShapeDtypeStruct((128, 256), BF),
        [pltpu.VMEM((128, 2048), BF)],
        2 * 128 * 2048 * 256,
        2 << 20,
    )(pos, a0, a1, a2, w, b)


def project_kernel(dists, pos, own, other, w_ref, out_ref, *rest):
    codes = rest[-1]
    step = pl.program_id(0)
    layer, c = pos[0], pos[1]
    x, z = layer // NZ, layer % NZ

    @pl.when(step == 0)
    def _():
        for xh in range(2):
            codes[:, pl.ds(pl.multiple_of((xh * 2 + c) * 256, 256), 256)] = own[xh]
            codes[:, pl.ds(pl.multiple_of((xh * 2 + 1 - c) * 256, 256), 256)] = other[xh]
        if len(rest) > 1:
            rest[0][...] = codes[...].T

    target = lax.rem(z + step + dists, NZ)
    live = NZ + target >= layer

    @pl.when(live)
    def _():
        w = jnp.concatenate([w_ref[0, 0], w_ref[1, 0]], axis=1)
        prod = jnp.dot(codes[...], w, preferred_element_type=F32)
        out_ref[0, x] = jnp.where(target >= layer, prod[:, :128], 0.0).astype(out_ref.dtype)
        out_ref[0, 1 - x] = prod[:, 128:].astype(out_ref.dtype)

    @pl.when(jnp.logical_not(live))
    def _():
        out_ref[...] = jnp.zeros_like(out_ref)


def project(pos, own, other, w, first, count, transposed):
    outs = [jax.ShapeDtypeStruct((count, 2, 512, 128), F32)]
    specs = [pl.BlockSpec((1, 2, 512, 128), lambda i, pos: (i, 0, 0, 0))]
    if transposed:
        outs.append(jax.ShapeDtypeStruct((1024, 512), BF))
        specs.append(whole((1024, 512)))
    return call(
        functools.partial(project_kernel, first),
        (count,),
        [
            whole((2, 512, 256)),
            whole((2, 512, 256)),
            pl.BlockSpec(
                (2, 1, 1024, 128),
                lambda i, pos: (0, lax.rem(pos[0] + i + first, NZ), 0, 0),
            ),
        ],
        specs,
        outs,
        [pltpu.VMEM((512, 1024), BF)],
        count * 2 * 512 * 1024 * 256,
        count << 20,
    )(pos, own, other, w)


def backprop_kernel(dists, first_call, pos, *refs):
    n = len(dists)
    errs, rest = refs[:n], refs[n:]
    codes_t, w_ref = rest[0], rest[1]
    rest = rest[2:] if first_call else rest[4:]
    dec_ref, acc_ref, err = rest
    if not first_call:
        acc_in = refs[n + 3]
    step = pl.program_id(0)
    layer = pos[0]
    x, z = layer // NZ, layer % NZ

    if first_call:

        @pl.when(step == 0)
        def _():
            acc_ref[...] = jnp.zeros_like(acc_ref)

    else:

        @pl.when(step == 0)
        def _():
            acc_ref[...] = acc_in[...]

    target = z
    for k, d in enumerate(dists):
        target = jnp.where(step == k, lax.rem(z + d, NZ), target)
    live = NZ + target >= layer

    @pl.when(live)
    def _():
        for k in range(n):

            @pl.when(step == k)
            def _(k=k):
                zero = jnp.zeros((512, 128), BF)
                err[:, :128] = jnp.where(target >= layer, errs[k][x], zero)
                err[:, 128:] = errs[k][1 - x]

        e = err[...]
        grad = jnp.dot(codes_t[...], e, preferred_element_type=F32)
        dec_ref[0, 0] = grad[:, :128].astype(BF)
        dec_ref[1, 0] = grad[:, 128:].astype(BF)
        w = jnp.concatenate([w_ref[0, 0], w_ref[1, 0]], axis=1)
        acc_ref[...] += lax.dot_general(
            e, w, (((1,), (1,)), ((), ())), preferred_element_type=F32
        )

    @pl.when(jnp.logical_not(live))
    def _():
        dec_ref[...] = jnp.zeros_like(dec_ref)


def backprop(pos, errs, dists, codes_t, w, carry=None):
    n = len(dists)

    def z_map(i, pos):
        target = pos[0]
        for k, d in enumerate(dists):
            target = jnp.where(i == k, pos[0] + d, target)
        return (0, lax.rem(target, NZ), 0, 0)

    blocks = pl.BlockSpec((2, 1, 1024, 128), z_map)
    specs = [whole((2, 512, 128))] * n + [whole((1024, 512)), blocks]
    args = [pos, *errs, codes_t, w]
    aliases = {}
    if carry is not None:
        specs += [pl.BlockSpec(memory_space=pl.ANY), whole((512, 1024))]
        args += list(carry)
        aliases = {n + 3: 0}
    return call(
        functools.partial(backprop_kernel, dists, carry is None),
        (n,),
        specs,
        [blocks, whole((512, 1024))],
        [
            jax.ShapeDtypeStruct((2, NZ, 1024, 128), BF),
            jax.ShapeDtypeStruct((512, 1024), F32),
        ],
        [pltpu.VMEM((512, 256), BF)],
        n * 4 * 512 * 1024 * 256,
        n << 20,
        aliases,
    )(*args)


def local(acts, w_enc, b_enc, w_dec, targets):
    layer = lax.axis_index("layer")
    tok = lax.axis_index("tok")
    pos = jnp.stack([layer, tok % 2, tok % 4]).astype(jnp.int32)

    a0 = acts[0]
    a1 = permute(a0, CORE_SWAP)
    a2 = permute(jnp.stack([a0, a1]), XHI_SWAP)
    w_cols = jnp.transpose(w_enc[0].reshape(128, 4, 256), (1, 0, 2))
    w_rows = swap_blocks(w_cols, G_PLANE).reshape(512, 256)
    w_full = spread(w_rows, G_Y).reshape(2048, 256)
    block = encode(pos, a0, a1, a2, w_full, b_enc)
    own = spread(block, G_CHIP).reshape(2, 512, 256)
    other = permute(own, CORE_SWAP)

    w = w_dec[0].reshape(2, NZ, 1024, 128)
    (far,) = project(pos, own, other, w, 4, 1, False)
    near, codes_t = project(pos, own, other, w, 5, 7, True)
    parts = {d: near[d - 5] for d in (5, 6, 7)}
    parts.update({d: near[d + 3] for d in (0, 1, 2, 3)})
    up = permute(far[0, 0].astype(BF), Z_UP).astype(F32)
    down = permute(far[0, 1].astype(BF), Z_DOWN).astype(F32)
    up = jnp.stack([parts[3][0] + up, parts[3][1]])
    down = jnp.stack([parts[5][0], parts[5][1] + down])
    for hop in (2, 1, 0):
        up = permute(up.astype(BF), Z_UP).astype(F32)
        down = permute(down.astype(BF), Z_DOWN).astype(F32)
        if hop:
            up = up + parts[hop]
            down = down + parts[NZ - hop]
    total = parts[0] + up + down
    cross = permute(total[1].astype(BF), X_SWAP).astype(F32)
    err = (total[0] + cross - targets[0].astype(F32)).astype(BF)

    pair = jnp.stack([err, permute(err, X_SWAP)])
    ups, downs = [pair], [pair]
    for _ in range(3):
        ups.append(permute(ups[-1], Z_UP))
        downs.append(permute(downs[-1], Z_DOWN))
    opposite = jnp.stack(
        [permute(ups[-1][0], Z_UP), permute(downs[-1][1], Z_DOWN)]
    )
    carry = backprop(
        pos,
        [pair, ups[1], downs[1], ups[2], downs[2]],
        (0, 7, 1, 6, 2),
        codes_t,
        w,
    )
    dec_grad, partial = backprop(
        pos, [ups[3], downs[3], opposite], (5, 3, 4), codes_t, w, carry
    )

    halves = partial.reshape(8, 2, 32, 1024)
    core = tok % 2
    keep = lax.dynamic_index_in_dim(halves, core, 1, keepdims=False)
    give = lax.dynamic_index_in_dim(halves, 1 - core, 1, keepdims=False)
    chip = keep + permute(give, CORE_SWAP)
    chip = chip.reshape(4, 2, 32, 1024).transpose(1, 0, 2, 3).reshape(8, 32, 1024)
    shares = swap_blocks(chip.astype(BF), G_CHIP).astype(F32)
    code_grad = jnp.sum(shares, axis=0)
    return code_grad[None], dec_grad.reshape(1, NL, 1024, 128)


def solution(mesh):
    return jax.shard_map(
        local,
        mesh=mesh,
        in_specs=(
            P("layer", "tok", None),
            P("layer", "tok", None),
            P("layer", None),
            P("layer", None, None, "tok"),
            P("layer", None, "tok"),
        ),
        out_specs=(P("layer", "tok", None), P("layer", None, None, "tok")),
        check_vma=False,
    )
```

time: 522 us -> 167 us (0.32)
  waiting for transfers between devices: 345 us -> 66.1 us
  matrix products: 108 us -> 0 us
  local copies, waits for them, and re-layouts: 49.5 us -> 7.92 us
  blocking collectives: 0 us -> 39.1 us
  starting transfers between devices: 0.16 us -> 30.4 us
  Pallas kernels: 0 us -> 17 us
  between operations: 13.8 us -> 0.93 us
    psum x1 -> x0, waiting for transfers between devices: 148 us -> none  [local(): errors = lax.psum(partials, 'layer')]
    all_gather x2 -> x0, waiting for transfers between devices: 113 us -> none  [the longest x1 65.3 us: local(): lax.all_gather(w_enc, 'tok', axis=1, tiled=True)[0]]
    dot_general x46 -> x0, matrix products: 108 us -> none  [the longest x15 44.5 us: backprop_advance(): lax.dot_general(source_wide, error_block, (((0,), (0,)), ((), ())), preci...]
    reduce_scatter x1 -> x0, waiting for transfers between devices: 82.9 us -> none  [local(): lax.psum_scatter(code_partial, 'tok', scatter_dimension=0, tiled=True)]
    ppermute x0 -> x22, waiting for transfers between devices: none -> 62.7 us  [permute(): return lax.ppermute(x, AXES, pairs)]
    all_to_all x0 -> x3, blocking collectives: none -> 39.1 us  [swap_blocks(): return lax.all_to_all(x, 'tok', 0, 0, axis_index_groups=groups)]
    dynamic_update_slice x60 -> x0, local copies, waits for them, and re-layouts: 26.1 us -> none  [the longest x30 13.4 us: backprop_advance(): lax.dynamic_update_index_in_dim(weight_grads, block_grad.astype(jnp.bfloa...]
    ppermute x0 -> x22, starting transfers between devices: none -> 25.9 us  [permute(): return lax.ppermute(x, AXES, pairs)]
  transfers between devices with their start and end apart: 4 -> 23, of which waited for: 4 -> 16; matrix products, arithmetic and copies ran while one was open for 0% -> 0% of each run, Pallas kernels for 0% -> 7%
where the time goes in v1:
time: 167 us; the launch traced here: 165 us
  waiting for transfers between devices  66.1 us (40%)
  blocking collectives  39.1 us (23%)
  starting transfers between devices  30.4 us (18%)
  Pallas kernels  17 us (10%)
  local copies, waits for them, and re-layouts  7.92 us (5%)
  other arithmetic  3.11 us (2%)
    ppermute x22, waiting for transfers between devices, permute(): return lax.ppermute(x, AXES, pairs)  62.7 us
    all_to_all x3, blocking collectives, swap_blocks(): return lax.all_to_all(x, 'tok', 0, 0, axis_index_groups=groups)  39.1 us
    ppermute x22, starting transfers between devices, permute(): return lax.ppermute(x, AXES, pairs)  25.9 us
    pallas_call x2, Pallas kernels, backprop(): call(functools.partial(backprop_kernel, dists, carry is None), (n,), spec...  10.2 us
    unnamed x15, local copies, waits for them, and re-layouts  6.49 us
    pallas_call x2, Pallas kernels, project(): call(functools.partial(project_kernel, first), (count,), [whole((2, 512,...  5.98 us
    all_to_all x1, starting transfers between devices, swap_blocks(): return lax.all_to_all(x, 'tok', 0, 0, axis_index_groups=groups)  4.46 us
    all_to_all x1, waiting for transfers between devices, swap_blocks(): return lax.all_to_all(x, 'tok', 0, 0, axis_index_groups=groups)  3.4 us
  transfers between devices with their start and end apart: 23, of which 16 were waited for; matrix products, arithmetic and copies ran while one was open for 0% of the time, Pallas kernels for 7%

profile of v1, /device:TPU:32, one launch (start us, length us, event | category | flops | bytes accessed | tf_op | source)
XLA Modules:
  0.0 164.6 jit_solution(12278706712894558881)
XLA Ops:
  0.6 1.2 copy.8
  1.8 11.6 %all_to_all.20 = bf16[4,128,256]{1,2,0:T(8,128)(2,1)S(1)} all-to-all(bf16[4,128,256]{1,2,0:T(8,128)(2,1)S(1)} %bitcast.107), channel_id=1, replica_groups={{0,1,2,3},{4,5,6,7},{8,9,10,11},{12,13,14,15},{16,17,18,19},{20,21,22,2..., dimensions={0} | all-to-all | bytes 524288 | tf_op jit(solution)/shard_map/all_to_all | solution.py:40
  13.4 0.1 copy.9
  13.6 1.0 broadcast_in_dim.17
  14.6 4.5 %all-to-all-start.1 = ((bf16[4,512,256]{2,1,0:T(8,128)(2,1)}), bf16[4,512,256]{2,1,0:T(8,128)(2,1)S(1)}, u32[]{:S(2)}, u32[]{:S(2)}) async-start(bf16[4,512,256]{2,1,0:T(8,128)(2,1)} %broadcast_in_dim.17), calls=%async_computation.1 | async-start | bytes 2097152 | tf_op jit(solution)/shard_map/all_to_all | solution.py:40
  19.1 0.0 collective-permute-start
  19.1 1.3 collective-permute-done.a1
  20.4 0.5 collective-permute-start.1
  20.9 0.1 pad_add_fusion.pos
  21.0 9.4 %collective-permute-done.1.a2 = bf16[2,32,2048]{2,1,0:T(8,128)(2,1)S(1)} collective-permute-done((bf16[2,32,2048]{2,1,0:T(8,128)(2,1)S(1)}, bf16[2,32,2048]{2,1,0:T(8,128)(2,1)S(1)}, u32[]{:S(2)}, u32[]{:S(2)}) %collective-permute-start.1) | collective-permute-done | bytes 262176 | tf_op jit(solution)/shard_map/ppermute | solution.py:36
  30.4 3.4 %all-to-all-done.1 = bf16[4,512,256]{2,1,0:T(8,128)(2,1)S(1)} async-done(((bf16[4,512,256]{2,1,0:T(8,128)(2,1)}), bf16[4,512,256]{2,1,0:T(8,128)(2,1)S(1)}, u32[]{:S(2)}, u32[]{:S(2)}) %all-to-all-start.1) | async-done | bytes 1048608 | tf_op jit(solution)/shard_map/all_to_all | solution.py:40
  33.8 0.9 shard_map.68
  34.7 13.0 %all_to_all.21 = bf16[8,128,256]{2,1,0:T(8,128)(2,1)S(1)} all-to-all(bf16[8,128,256]{2,1,0:T(8,128)(2,1)S(1)} %broadcast_in_dim.18), channel_id=1, replica_groups={{0,4,8,12,2,6,10,14},{1,5,9,13,3,7,11,15},{16,20,24,28,18,22,26,30},{17..., dimensions={0} | all-to-all | bytes 1048576 | tf_op jit(solution)/shard_map/all_to_all | solution.py:40
  47.7 0.0 collective-permute-start.2
  47.7 1.9 %collective-permute-done.2.other = bf16[2,512,256]{2,1,0:T(8,128)(2,1)S(1)} collective-permute-done((bf16[2,512,256]{2,1,0:T(8,128)(2,1)S(1)}, bf16[2,512,256]{2,1,0:T(8,128)(2,1)S(1)}, u32[]{:S(2)}, u32[]{:S(2)}) %collective-permute-start.2) | collective-permute-done | bytes 524320 | tf_op jit(solution)/shard_map/ppermute | solution.py:36
  49.6 2.2 %copy-done = bf16[1,16,1024,128]{3,2,1,0:T(8,128)(2,1)S(1)} copy-done((bf16[1,16,1024,128]{3,2,1,0:T(8,128)(2,1)S(1)}, bf16[1,16,1024,128]{3,2,1,0:T(8,128)(2,1)}, u32[]{:S(2)}) %copy-start) | copy-done | bytes 4194328
  51.8 1.2 shard_map.70
  53.1 2.0 %collective-permute-start.3 = (bf16[512,128]{1,0:T(8,128)(2,1)S(1)}, bf16[512,128]{1,0:T(8,128)(2,1)S(1)}, u32[]{:S(2)}, u32[]{:S(2)}) collective-permute-start(bf16[512,128]{1,0:T(8,128)(2,1)S(1)} %get-tuple-element.22), channel_id=1, source_target_pairs={{0,16},{1,17},{2,18},{3,19},{4,20},{5,21},{6,22},{7,23},{8,24},{9,... | collective-permute-start | bytes 393224 | tf_op jit(solution)/shard_map/ppermute | solution.py:36
  55.1 0.1 collective-permute-start.7
  55.2 4.8 %shard_map.69 = (f32[7,2,512,128]{3,2,1,0:T(8,128)S(1)}, bf16[1024,512]{1,0:T(8,128)(2,1)S(1)}) custom-call(s32[3]{0:T(128)S(1)} %pad_add_fusion.pos, bf16[2,512,256]{2,1,0:T(8,128)(2,1)S(1)} %bitcast.97, bf16[2,512,256]{2,1,0:T(8,128)(2,1)S(1)} %collective-permute-done.2.other, bf16[2,8,1024,128]{3,2,1,0:T(8,128)(2,1)S(1)} %bitcast.91), custom_call_target="tpu_custom_call" | custom-call | flops 1879048192 | bytes 7340032 | tf_op jit(solution)/shard_map/pallas_call | solution.py:130
  60.0 0.3 convert.26
  60.4 0.1 collective-permute-done.7
  60.5 0.1 fusion.11
  60.6 0.0 copy-start.6
  60.6 4.0 %collective-permute-start.8 = (bf16[2,512,128]{2,1,0:T(8,128)(2,1)S(1)}, bf16[2,512,128]{2,1,0:T(8,128)(2,1)S(1)}, u32[]{:S(2)}, u32[]{:S(2)}) collective-permute-start(bf16[2,512,128]{2,1,0:T(8,128)(2,1)S(1)} %pad_maximum_fusion.2), channel_id=1, source_target_pairs={{0,112},{1,113},{2,114},{3,115},{4,116},{5,117},{6,118},{7,119},{8... | collective-permute-start | bytes 786440 | tf_op jit(solution)/shard_map/ppermute | solution.py:36
  64.7 0.1 collective-permute-start.4
  64.7 5.5 %collective-permute-done.8 = bf16[2,512,128]{2,1,0:T(8,128)(2,1)S(1)} collective-permute-done((bf16[2,512,128]{2,1,0:T(8,128)(2,1)S(1)}, bf16[2,512,128]{2,1,0:T(8,128)(2,1)S(1)}, u32[]{:S(2)}, u32[]{:S(2)}) %collective-permute-start.8) | collective-permute-done | bytes 262176 | tf_op jit(solution)/shard_map/ppermute | solution.py:36
  70.2 2.3 %collective-permute-done.4 = bf16[2,512,128]{2,1,0:T(8,128)(2,1)S(1)} collective-permute-done((bf16[2,512,128]{2,1,0:T(8,128)(2,1)S(1)}, bf16[2,512,128]{2,1,0:T(8,128)(2,1)S(1)}, u32[]{:S(2)}, u32[]{:S(2)}) %collective-permute-start.4) | collective-permute-done | bytes 262176 | tf_op jit(solution)/shard_map/ppermute | solution.py:36
  72.5 0.1 fusion.4
  72.6 0.4 collective-permute-start.5
  73.0 2.7 %collective-permute-start.9 = (bf16[2,512,128]{2,1,0:T(8,128)(2,1)S(1)}, bf16[2,512,128]{2,1,0:T(8,128)(2,1)S(1)}, u32[]{:S(2)}, u32[]{:S(2)}) collective-permute-start(bf16[2,512,128]{2,1,0:T(8,128)(2,1)S(1)} %get-tuple-element.17), channel_id=1, source_target_pairs={{0,112},{1,113},{2,114},{3,115},{4,116},{5,117},{6,118},{7,119},{8... | collective-permute-start | bytes 786440 | tf_op jit(solution)/shard_map/ppermute | solution.py:36
  75.7 4.8 %collective-permute-done.5 = bf16[2,512,128]{2,1,0:T(8,128)(2,1)S(1)} collective-permute-done((bf16[2,512,128]{2,1,0:T(8,128)(2,1)S(1)}, bf16[2,512,128]{2,1,0:T(8,128)(2,1)S(1)}, u32[]{:S(2)}, u32[]{:S(2)}) %collective-permute-start.5) | collective-permute-done | bytes 262176 | tf_op jit(solution)/shard_map/ppermute | solution.py:36
  80.5 0.0 collective-permute-done.9
  80.5 0.1 fusion.3
  80.6 3.0 %collective-permute-start.10 = (bf16[2,512,128]{2,1,0:T(8,128)(2,1)S(1)}, bf16[2,512,128]{2,1,0:T(8,128)(2,1)S(1)}, u32[]{:S(2)}, u32[]{:S(2)}) collective-permute-start(bf16[2,512,128]{2,1,0:T(8,128)(2,1)S(1)} %get-tuple-element.15), channel_id=1, source_target_pairs={{0,112},{1,113},{2,114},{3,115},{4,116},{5,117},{6,118},{7,119},{8... | collective-permute-start | bytes 786440 | tf_op jit(solution)/shard_map/ppermute | solution.py:36
  83.7 0.0 collective-permute-start.6
  83.7 3.9 %collective-permute-done.10 = bf16[2,512,128]{2,1,0:T(8,128)(2,1)S(1)} collective-permute-done((bf16[2,512,128]{2,1,0:T(8,128)(2,1)S(1)}, bf16[2,512,128]{2,1,0:T(8,128)(2,1)S(1)}, u32[]{:S(2)}, u32[]{:S(2)}) %collective-permute-start.10) | collective-permute-done | bytes 262176 | tf_op jit(solution)/shard_map/ppermute | solution.py:36
  87.5 3.4 %collective-permute-done.6 = bf16[2,512,128]{2,1,0:T(8,128)(2,1)S(1)} collective-permute-done((bf16[2,512,128]{2,1,0:T(8,128)(2,1)S(1)}, bf16[2,512,128]{2,1,0:T(8,128)(2,1)S(1)}, u32[]{:S(2)}, u32[]{:S(2)}) %collective-permute-start.6) | collective-permute-done | bytes 262176 | tf_op jit(solution)/shard_map/ppermute | solution.py:36
  91.0 0.1 fusion.5
  91.1 0.1 collective-permute-start.11
  91.2 5.7 %collective-permute-done.11 = bf16[512,128]{1,0:T(8,128)(2,1)S(1)} collective-permute-done((bf16[512,128]{1,0:T(8,128)(2,1)S(1)}, bf16[512,128]{1,0:T(8,128)(2,1)S(1)}, u32[]{:S(2)}, u32[]{:S(2)}) %collective-permute-start.11) | collective-permute-done | bytes 131104 | tf_op jit(solution)/shard_map/ppermute | solution.py:36
  96.9 0.1 fusion.8
  96.9 0.6 collective-permute-start.12
  97.5 4.7 %collective-permute-done.12 = bf16[512,128]{1,0:T(8,128)(2,1)S(1)} collective-permute-done((bf16[512,128]{1,0:T(8,128)(2,1)S(1)}, bf16[512,128]{1,0:T(8,128)(2,1)S(1)}, u32[]{:S(2)}, u32[]{:S(2)}) %collective-permute-start.12) | collective-permute-done | bytes 131104 | tf_op jit(solution)/shard_map/ppermute | solution.py:36
  102.2 0.1 collective-permute-start.13
  102.3 3.0 %collective-permute-start.16 = (bf16[2,512,128]{2,1,0:T(8,128)(2,1)S(1)}, bf16[2,512,128]{2,1,0:T(8,128)(2,1)S(1)}, u32[]{:S(2)}, u32[]{:S(2)}) collective-permute-start(bf16[2,512,128]{2,1,0:T(8,128)(2,1)S(1)} %pad_maximum_fusion.3.refs_0_), channel_id=1, source_target_pairs={{0,112},{1,113},{2,114},{3,115},{4,116},{5,117},{6,118},{7,119},{8... | collective-permute-start | bytes 786440 | tf_op jit(solution)/shard_map/ppermute | solution.py:36
  105.3 6.7 %collective-permute-done.13.refs_1_ = bf16[2,512,128]{2,1,0:T(8,128)(2,1)S(1)} collective-permute-done((bf16[2,512,128]{2,1,0:T(8,128)(2,1)S(1)}, bf16[2,512,128]{2,1,0:T(8,128)(2,1)S(1)}, u32[]{:S(2)}, u32[]{:S(2)}) %collective-permute-start.13) | collective-permute-done | bytes 262176 | tf_op jit(solution)/shard_map/ppermute | solution.py:36
  112.0 0.0 collective-permute-start.14
  112.0 3.0 %collective-permute-start.17 = (bf16[2,512,128]{2,1,0:T(8,128)(2,1)S(1)}, bf16[2,512,128]{2,1,0:T(8,128)(2,1)S(1)}, u32[]{:S(2)}, u32[]{:S(2)}) collective-permute-start(bf16[2,512,128]{2,1,0:T(8,128)(2,1)S(1)} %collective-permute-done.16.refs_2_), channel_id=1, source_target_pairs={{0,112},{1,113},{2,114},{3,115},{4,116},{5,117},{6,118},{7,119},{8... | collective-permute-start | bytes 786440 | tf_op jit(solution)/shard_map/ppermute | solution.py:36
  114.9 5.9 %collective-permute-done.14.refs_3_ = bf16[2,512,128]{2,1,0:T(8,128)(2,1)S(1)} collective-permute-done((bf16[2,512,128]{2,1,0:T(8,128)(2,1)S(1)}, bf16[2,512,128]{2,1,0:T(8,128)(2,1)S(1)}, u32[]{:S(2)}, u32[]{:S(2)}) %collective-permute-start.14) | collective-permute-done | bytes 262176 | tf_op jit(solution)/shard_map/ppermute | solution.py:36
  120.9 3.0 %collective-permute-start.18 = (bf16[2,512,128]{2,1,0:T(8,128)(2,1)S(1)}, bf16[2,512,128]{2,1,0:T(8,128)(2,1)S(1)}, u32[]{:S(2)}, u32[]{:S(2)}) collective-permute-start(bf16[2,512,128]{2,1,0:T(8,128)(2,1)S(1)} %collective-permute-done.17.refs_4_), channel_id=1, source_target_pairs={{0,112},{1,113},{2,114},{3,115},{4,116},{5,117},{6,118},{7,119},{8... | collective-permute-start | bytes 786440 | tf_op jit(solution)/shard_map/ppermute | solution.py:36
  123.8 4.3 %collective-permute-done.15.refs_0_ = bf16[2,512,128]{2,1,0:T(8,128)(2,1)S(1)} collective-permute-done((bf16[2,512,128]{2,1,0:T(8,128)(2,1)S(1)}, bf16[2,512,128]{2,1,0:T(8,128)(2,1)S(1)}, u32[]{:S(2)}, u32[]{:S(2)}) %collective-permute-start.15) | collective-permute-done | bytes 262176 | tf_op jit(solution)/shard_map/ppermute | solution.py:36
  128.2 0.1 collective-permute-start.19
  128.3 3.3 %collective-permute-start.20 = (bf16[512,128]{1,0:T(8,128)(2,1)S(1)}, bf16[512,128]{1,0:T(8,128)(2,1)S(1)}, u32[]{:S(2)}, u32[]{:S(2)}) collective-permute-start(bf16[512,128]{1,0:T(8,128)(2,1)S(1)} %slice_bitcast_fusion.1), channel_id=1, source_target_pairs={{0,112},{1,113},{2,114},{3,115},{4,116},{5,117},{6,118},{7,119},{8... | collective-permute-start | bytes 393224 | tf_op jit(solution)/shard_map/ppermute | solution.py:36
  131.6 2.2 %copy-done.1 = bf16[1,16,1024,128]{3,2,1,0:T(8,128)(2,1)S(1)} copy-done((bf16[1,16,1024,128]{3,2,1,0:T(8,128)(2,1)S(1)}, bf16[1,16,1024,128]{3,2,1,0:T(8,128)(2,1)}, u32[]{:S(2)}) %copy-start.1) | copy-done | bytes 4194328
  133.8 6.0 %shard_map.71 = (bf16[2,8,1024,128]{3,2,1,0:T(8,128)(2,1)}, f32[512,1024]{1,0:T(8,128)S(1)}) custom-call(s32[3]{0:T(128)S(1)} %pad_add_fusion.pos, bf16[2,512,128]{2,1,0:T(8,128)(2,1)S(1)} %pad_maximum_fusion.3.refs_0_, bf16[2,512,128]{2,1,0:T(8,128)(2,1)S(1)} %collective-permute-done.13.refs_1_, bf16[2,512,128]{2,1,0:T(8,128)(2,1)S(1)} %collective-permute-done.16.refs_2_, ...), custom_call_target="tpu_custom_call" | custom-call | flops 2684354560 | bytes 5242880 | tf_op jit(solution)/shard_map/pallas_call | solution.py:219
  139.9 0.9 copy-done.3
  140.8 4.1 %shard_map.72 = (bf16[2,8,1024,128]{3,2,1,0:T(8,128)(2,1)}, f32[512,1024]{1,0:T(8,128)S(1)}) custom-call(s32[3]{0:T(128)S(1)} %pad_add_fusion.pos, bf16[2,512,128]{2,1,0:T(8,128)(2,1)S(1)} %collective-permute-done.15.refs_0_, bf16[2,512,128]{2,1,0:T(8,128)(2,1)S(1)} %copy-done.3, ...), custom_call_target="tpu_custom_call", output_to_operand_aliasing={{0}: (6, {})} | custom-call | flops 1610612736 | bytes 3145728 | tf_op jit(solution)/shard_map/pallas_call | solution.py:219
  145.0 0.1 dynamic-slice_bitcast_fusion
  145.1 0.1 collective-permute-start.21
  145.2 2.8 %collective-permute-done.21 = f32[8,32,1024]{2,1,0:T(8,128)} collective-permute-done((f32[8,32,1024]{2,1,0:T(8,128)S(1)}, f32[8,32,1024]{2,1,0:T(8,128)}, u32[]{:S(2)}, u32[]{:S(2)}) %collective-permute-start.21) | collective-permute-done | bytes 1048608 | tf_op jit(solution)/shard_map/ppermute | solution.py:36
  147.9 1.4 fusion
  149.3 14.5 %all_to_all.22 = bf16[8,32,1024]{2,1,0:T(8,128)(2,1)S(1)} all-to-all(bf16[8,32,1024]{2,1,0:T(8,128)(2,1)S(1)} %bitcast.104), channel_id=1, replica_groups={{0,4,8,12,2,6,10,14},{1,5,9,13,3,7,11,15},{16,20,24,28,18,22,26,30},{17..., dimensions={0} | all-to-all | bytes 1048576 | tf_op jit(solution)/shard_map/all_to_all | solution.py:40
  163.9 0.7 convert_reduce_fusion
  (30 shorter events, 0.4 us)
Async XLA Ops:
  0.6 18.4 %copy-start.4 = (bf16[1,32,2048]{2,1,0:T(8,128)(2,1)S(1)}, bf16[1,32,2048]{2,1,0:T(8,128)(2,1)}, u32[]{:S(2)}) copy-start(bf16[1,32,2048]{2,1,0:T(8,128)(2,1)} %param.5) | copy-start | bytes 393220
  0.6 33.2 %copy-start.5 = (f32[1,1024]{1,0:T(1,128)S(1)}, f32[1,1024]{1,0:T(1,128)}, u32[]{:S(2)}) copy-start(f32[1,1024]{1,0:T(1,128)} %b_ref.1) | copy-start | bytes 12292
  14.6 19.2 %all-to-all-start.1 = ((bf16[4,512,256]{2,1,0:T(8,128)(2,1)}), bf16[4,512,256]{2,1,0:T(8,128)(2,1)S(1)}, u32[]{:S(2)}, u32[]{:S(2)}) async-start(bf16[4,512,256]{2,1,0:T(8,128)(2,1)} %broadcast_in_dim.17), calls=%async_computation.1 | async-start | bytes 2097152 | tf_op jit(solution)/shard_map/all_to_all | solution.py:40
  19.1 1.3 collective-permute-start
  20.4 9.9 %collective-permute-start.1 = (bf16[2,32,2048]{2,1,0:T(8,128)(2,1)S(1)}, bf16[2,32,2048]{2,1,0:T(8,128)(2,1)S(1)}, u32[]{:S(2)}, u32[]{:S(2)}) collective-permute-start(bf16[2,32,2048]{2,1,0:T(8,128)(2,1)S(1)} %pad_maximum_fusion), channel_id=1, source_target_pairs={{0,2},{1,3},{2,0},{3,1},{4,6},{5,7},{6,4},{7,5},{8,10},{9,11},{10,... | collective-permute-start | bytes 786440 | tf_op jit(solution)/shard_map/ppermute | solution.py:36
  47.7 1.9 %collective-permute-start.2 = (bf16[2,512,256]{2,1,0:T(8,128)(2,1)S(1)}, bf16[2,512,256]{2,1,0:T(8,128)(2,1)S(1)}, u32[]{:S(2)}, u32[]{:S(2)}) collective-permute-start(bf16[2,512,256]{2,1,0:T(8,128)(2,1)S(1)} %bitcast.95), channel_id=1, source_target_pairs={{0,1},{1,0},{2,3},{3,2},{4,5},{5,4},{6,7},{7,6},{8,9},{9,8},{10,11... | collective-permute-start | bytes 1572872 | tf_op jit(solution)/shard_map/ppermute | solution.py:36
  49.6 2.2 %copy-start = (bf16[1,16,1024,128]{3,2,1,0:T(8,128)(2,1)S(1)}, bf16[1,16,1024,128]{3,2,1,0:T(8,128)(2,1)}, u32[]{:S(2)}) copy-start(bf16[1,16,1024,128]{3,2,1,0:T(8,128)(2,1)} %param.8) | copy-start | bytes 12582916
  53.1 7.3 %collective-permute-start.3 = (bf16[512,128]{1,0:T(8,128)(2,1)S(1)}, bf16[512,128]{1,0:T(8,128)(2,1)S(1)}, u32[]{:S(2)}, u32[]{:S(2)}) collective-permute-start(bf16[512,128]{1,0:T(8,128)(2,1)S(1)} %get-tuple-element.22), channel_id=1, source_target_pairs={{0,16},{1,17},{2,18},{3,19},{4,20},{5,21},{6,22},{7,23},{8,24},{9,... | collective-permute-start | bytes 393224 | tf_op jit(solution)/shard_map/ppermute | solution.py:36
  55.1 5.4 %collective-permute-start.7 = (bf16[512,128]{1,0:T(8,128)(2,1)S(1)}, bf16[512,128]{1,0:T(8,128)(2,1)S(1)}, u32[]{:S(2)}, u32[]{:S(2)}) collective-permute-start(bf16[512,128]{1,0:T(8,128)(2,1)S(1)} %get-tuple-element.23), channel_id=1, source_target_pairs={{0,112},{1,113},{2,114},{3,115},{4,116},{5,117},{6,118},{7,119},{8... | collective-permute-start | bytes 393224 | tf_op jit(solution)/shard_map/ppermute | solution.py:36
  60.6 36.3 %copy-start.6 = (bf16[1,512,128]{2,1,0:T(8,128)(2,1)S(1)}, bf16[1,512,128]{2,1,0:T(8,128)(2,1)}, u32[]{:S(2)}) copy-start(bf16[1,512,128]{2,1,0:T(8,128)(2,1)} %param.9) | copy-start | bytes 393220
  60.6 9.6 %collective-permute-start.8 = (bf16[2,512,128]{2,1,0:T(8,128)(2,1)S(1)}, bf16[2,512,128]{2,1,0:T(8,128)(2,1)S(1)}, u32[]{:S(2)}, u32[]{:S(2)}) collective-permute-start(bf16[2,512,128]{2,1,0:T(8,128)(2,1)S(1)} %pad_maximum_fusion.2), channel_id=1, source_target_pairs={{0,112},{1,113},{2,114},{3,115},{4,116},{5,117},{6,118},{7,119},{8... | collective-permute-start | bytes 786440 | tf_op jit(solution)/shard_map/ppermute | solution.py:36
  64.7 7.9 %collective-permute-start.4 = (bf16[2,512,128]{2,1,0:T(8,128)(2,1)S(1)}, bf16[2,512,128]{2,1,0:T(8,128)(2,1)S(1)}, u32[]{:S(2)}, u32[]{:S(2)}) collective-permute-start(bf16[2,512,128]{2,1,0:T(8,128)(2,1)S(1)} %pad_maximum_fusion.1), channel_id=1, source_target_pairs={{0,16},{1,17},{2,18},{3,19},{4,20},{5,21},{6,22},{7,23},{8,24},{9,... | collective-permute-start | bytes 786440 | tf_op jit(solution)/shard_map/ppermute | solution.py:36
  72.6 7.9 %collective-permute-start.5 = (bf16[2,512,128]{2,1,0:T(8,128)(2,1)S(1)}, bf16[2,512,128]{2,1,0:T(8,128)(2,1)S(1)}, u32[]{:S(2)}, u32[]{:S(2)}) collective-permute-start(bf16[2,512,128]{2,1,0:T(8,128)(2,1)S(1)} %get-tuple-element.16), channel_id=1, source_target_pairs={{0,16},{1,17},{2,18},{3,19},{4,20},{5,21},{6,22},{7,23},{8,24},{9,... | collective-permute-start | bytes 786440 | tf_op jit(solution)/shard_map/ppermute | solution.py:36
  73.0 7.5 %collective-permute-start.9 = (bf16[2,512,128]{2,1,0:T(8,128)(2,1)S(1)}, bf16[2,512,128]{2,1,0:T(8,128)(2,1)S(1)}, u32[]{:S(2)}, u32[]{:S(2)}) collective-permute-start(bf16[2,512,128]{2,1,0:T(8,128)(2,1)S(1)} %get-tuple-element.17), channel_id=1, source_target_pairs={{0,112},{1,113},{2,114},{3,115},{4,116},{5,117},{6,118},{7,119},{8... | collective-permute-start | bytes 786440 | tf_op jit(solution)/shard_map/ppermute | solution.py:36
  80.6 6.9 %collective-permute-start.10 = (bf16[2,512,128]{2,1,0:T(8,128)(2,1)S(1)}, bf16[2,512,128]{2,1,0:T(8,128)(2,1)S(1)}, u32[]{:S(2)}, u32[]{:S(2)}) collective-permute-start(bf16[2,512,128]{2,1,0:T(8,128)(2,1)S(1)} %get-tuple-element.15), channel_id=1, source_target_pairs={{0,112},{1,113},{2,114},{3,115},{4,116},{5,117},{6,118},{7,119},{8... | collective-permute-start | bytes 786440 | tf_op jit(solution)/shard_map/ppermute | solution.py:36
  83.7 7.3 %collective-permute-start.6 = (bf16[2,512,128]{2,1,0:T(8,128)(2,1)S(1)}, bf16[2,512,128]{2,1,0:T(8,128)(2,1)S(1)}, u32[]{:S(2)}, u32[]{:S(2)}) collective-permute-start(bf16[2,512,128]{2,1,0:T(8,128)(2,1)S(1)} %get-tuple-element.14), channel_id=1, source_target_pairs={{0,16},{1,17},{2,18},{3,19},{4,20},{5,21},{6,22},{7,23},{8,24},{9,... | collective-permute-start | bytes 786440 | tf_op jit(solution)/shard_map/ppermute | solution.py:36
  91.1 5.8 %collective-permute-start.11 = (bf16[512,128]{1,0:T(8,128)(2,1)S(1)}, bf16[512,128]{1,0:T(8,128)(2,1)S(1)}, u32[]{:S(2)}, u32[]{:S(2)}) collective-permute-start(bf16[512,128]{1,0:T(8,128)(2,1)S(1)} %fusion.13), channel_id=1, source_target_pairs={{0,128},{1,129},{2,130},{3,131},{4,132},{5,133},{6,134},{7,135},{8... | collective-permute-start | bytes 393224 | tf_op jit(solution)/shard_map/ppermute | solution.py:36
  96.9 5.2 %collective-permute-start.12 = (bf16[512,128]{1,0:T(8,128)(2,1)S(1)}, bf16[512,128]{1,0:T(8,128)(2,1)S(1)}, u32[]{:S(2)}, u32[]{:S(2)}) collective-permute-start(bf16[512,128]{1,0:T(8,128)(2,1)S(1)} %fusion.8), channel_id=1, source_target_pairs={{0,128},{1,129},{2,130},{3,131},{4,132},{5,133},{6,134},{7,135},{8... | collective-permute-start | bytes 393224 | tf_op jit(solution)/shard_map/ppermute | solution.py:36
  102.2 9.8 %collective-permute-start.13 = (bf16[2,512,128]{2,1,0:T(8,128)(2,1)S(1)}, bf16[2,512,128]{2,1,0:T(8,128)(2,1)S(1)}, u32[]{:S(2)}, u32[]{:S(2)}) collective-permute-start(bf16[2,512,128]{2,1,0:T(8,128)(2,1)S(1)} %pad_maximum_fusion.3.refs_0_), channel_id=1, source_target_pairs={{0,16},{1,17},{2,18},{3,19},{4,20},{5,21},{6,22},{7,23},{8,24},{9,... | collective-permute-start | bytes 786440 | tf_op jit(solution)/shard_map/ppermute | solution.py:36
  102.3 9.7 %collective-permute-start.16 = (bf16[2,512,128]{2,1,0:T(8,128)(2,1)S(1)}, bf16[2,512,128]{2,1,0:T(8,128)(2,1)S(1)}, u32[]{:S(2)}, u32[]{:S(2)}) collective-permute-start(bf16[2,512,128]{2,1,0:T(8,128)(2,1)S(1)} %pad_maximum_fusion.3.refs_0_), channel_id=1, source_target_pairs={{0,112},{1,113},{2,114},{3,115},{4,116},{5,117},{6,118},{7,119},{8... | collective-permute-start | bytes 786440 | tf_op jit(solution)/shard_map/ppermute | solution.py:36
  112.0 8.9 %collective-permute-start.14 = (bf16[2,512,128]{2,1,0:T(8,128)(2,1)S(1)}, bf16[2,512,128]{2,1,0:T(8,128)(2,1)S(1)}, u32[]{:S(2)}, u32[]{:S(2)}) collective-permute-start(bf16[2,512,128]{2,1,0:T(8,128)(2,1)S(1)} %collective-permute-done.13.refs_1_), channel_id=1, source_target_pairs={{0,16},{1,17},{2,18},{3,19},{4,20},{5,21},{6,22},{7,23},{8,24},{9,... | collective-permute-start | bytes 786440 | tf_op jit(solution)/shard_map/ppermute | solution.py:36
  112.0 8.9 %collective-permute-start.17 = (bf16[2,512,128]{2,1,0:T(8,128)(2,1)S(1)}, bf16[2,512,128]{2,1,0:T(8,128)(2,1)S(1)}, u32[]{:S(2)}, u32[]{:S(2)}) collective-permute-start(bf16[2,512,128]{2,1,0:T(8,128)(2,1)S(1)} %collective-permute-done.16.refs_2_), channel_id=1, source_target_pairs={{0,112},{1,113},{2,114},{3,115},{4,116},{5,117},{6,118},{7,119},{8... | collective-permute-start | bytes 786440 | tf_op jit(solution)/shard_map/ppermute | solution.py:36
  120.8 7.3 %collective-permute-start.15 = (bf16[2,512,128]{2,1,0:T(8,128)(2,1)S(1)}, bf16[2,512,128]{2,1,0:T(8,128)(2,1)S(1)}, u32[]{:S(2)}, u32[]{:S(2)}) collective-permute-start(bf16[2,512,128]{2,1,0:T(8,128)(2,1)S(1)} %collective-permute-done.14.refs_3_), channel_id=1, source_target_pairs={{0,16},{1,17},{2,18},{3,19},{4,20},{5,21},{6,22},{7,23},{8,24},{9,... | collective-permute-start | bytes 786440 | tf_op jit(solution)/shard_map/ppermute | solution.py:36
  120.9 7.4 %collective-permute-start.18 = (bf16[2,512,128]{2,1,0:T(8,128)(2,1)S(1)}, bf16[2,512,128]{2,1,0:T(8,128)(2,1)S(1)}, u32[]{:S(2)}, u32[]{:S(2)}) collective-permute-start(bf16[2,512,128]{2,1,0:T(8,128)(2,1)S(1)} %collective-permute-done.17.refs_4_), channel_id=1, source_target_pairs={{0,112},{1,113},{2,114},{3,115},{4,116},{5,117},{6,118},{7,119},{8... | collective-permute-start | bytes 786440 | tf_op jit(solution)/shard_map/ppermute | solution.py:36
  128.2 11.7 %collective-permute-start.19 = (bf16[512,128]{1,0:T(8,128)(2,1)S(1)}, bf16[512,128]{1,0:T(8,128)(2,1)S(1)}, u32[]{:S(2)}, u32[]{:S(2)}) collective-permute-start(bf16[512,128]{1,0:T(8,128)(2,1)S(1)} %slice_bitcast_fusion.2), channel_id=1, source_target_pairs={{0,16},{1,17},{2,18},{3,19},{4,20},{5,21},{6,22},{7,23},{8,24},{9,... | collective-permute-start | bytes 393224 | tf_op jit(solution)/shard_map/ppermute | solution.py:36
  128.3 11.6 %copy-start.2 = (bf16[2,512,128]{2,1,0:T(8,128)(2,1)}, bf16[2,512,128]{2,1,0:T(8,128)(2,1)S(1)}, u32[]{:S(2)}) copy-start(bf16[2,512,128]{2,1,0:T(8,128)(2,1)S(1)} %collective-permute-done.18.refs_1_) | copy-start | bytes 786436
  128.3 11.5 %collective-permute-start.20 = (bf16[512,128]{1,0:T(8,128)(2,1)S(1)}, bf16[512,128]{1,0:T(8,128)(2,1)S(1)}, u32[]{:S(2)}, u32[]{:S(2)}) collective-permute-start(bf16[512,128]{1,0:T(8,128)(2,1)S(1)} %slice_bitcast_fusion.1), channel_id=1, source_target_pairs={{0,112},{1,113},{2,114},{3,115},{4,116},{5,117},{6,118},{7,119},{8... | collective-permute-start | bytes 393224 | tf_op jit(solution)/shard_map/ppermute | solution.py:36
  131.6 2.2 %copy-start.1 = (bf16[1,16,1024,128]{3,2,1,0:T(8,128)(2,1)S(1)}, bf16[1,16,1024,128]{3,2,1,0:T(8,128)(2,1)}, u32[]{:S(2)}) copy-start(bf16[1,16,1024,128]{3,2,1,0:T(8,128)(2,1)} %param.8) | copy-start | bytes 12582916
  139.9 1.0 copy-start.3
  145.1 2.9 %collective-permute-start.21 = (f32[8,32,1024]{2,1,0:T(8,128)S(1)}, f32[8,32,1024]{2,1,0:T(8,128)}, u32[]{:S(2)}, u32[]{:S(2)}) collective-permute-start(f32[8,32,1024]{2,1,0:T(8,128)S(1)} %dynamic-slice_bitcast_fusion), channel_id=1, source_target_pairs={{0,1},{1,0},{2,3},{3,2},{4,5},{5,4},{6,7},{7,6},{8,9},{9,8},{10,11... | collective-permute-start | bytes 3145736 | tf_op jit(solution)/shard_map/ppermute | solution.py:36

commit v2 on v1

v2 whole, which is shorter than its diff:
```python
import functools

import jax
import jax.numpy as jnp
from jax import lax
from jax.experimental import pallas as pl
from jax.experimental.pallas import tpu as pltpu
from jax.sharding import PartitionSpec as P


BF = jnp.bfloat16
F32 = jnp.float32
AXES = ("layer", "tok")
NL, NT, NZ = 16, 16, 8


def _layer_perm(fn):
    return [(l * NT + t, fn(l) * NT + t) for l in range(NL) for t in range(NT)]


def _tok_perm(fn):
    return [(l * NT + t, l * NT + fn(t)) for l in range(NL) for t in range(NT)]


Z_UP = _layer_perm(lambda l: (l // NZ) * NZ + (l + 1) % NZ)
Z_DOWN = _layer_perm(lambda l: (l // NZ) * NZ + (l - 1) % NZ)
X_SWAP = _layer_perm(lambda l: l ^ NZ)
CORE_SWAP = _tok_perm(lambda t: t ^ 1)
XHI_SWAP = _tok_perm(lambda t: t ^ 2)

G_OUT = [[y * 4 + xh * 2 + c for y in range(4) for xh in range(2)] for c in range(2)]
G_CHIP = [[y * 4 + xh * 2 + c for xh in range(2) for y in range(4)] for c in range(2)]


def permute(x, pairs):
    return lax.ppermute(x, AXES, pairs)


def swap_blocks(x, groups):
    return lax.all_to_all(x, "tok", 0, 0, axis_index_groups=groups)


def call(kernel, in_specs, outs, scratch, flops, nbytes, aliases=None, room=16):
    return pl.pallas_call(
        kernel,
        in_specs=in_specs,
        out_specs=[o[1] for o in outs],
        out_shape=[o[0] for o in outs],
        scratch_shapes=scratch,
        input_output_aliases=aliases or {},
        cost_estimate=pl.CostEstimate(flops=flops, bytes_accessed=nbytes, transcendentals=0),
        compiler_params=pltpu.CompilerParams(vmem_limit_bytes=room << 20),
    )


SMEM = pl.BlockSpec(memory_space=pltpu.SMEM)
VMEM = pl.BlockSpec(memory_space=pltpu.VMEM)
HBM = pl.BlockSpec(memory_space=pltpu.HBM)


def in_vmem(shape, dtype):
    return (jax.ShapeDtypeStruct(shape, dtype), VMEM)


def in_hbm(shape, dtype):
    return (jax.ShapeDtypeStruct(shape, dtype), HBM)


def columns_kernel(w_ref, out_ref):
    for t in range(NT):
        q = t % 4
        out_ref[t] = w_ref[:, q * 256 : (q + 1) * 256]


def columns(w):
    return call(columns_kernel, [VMEM], [in_vmem((NT, 128, 256), BF)], [], 0, 5 << 18)(w)[0]


def encode_kernel(pos, a0, a1, a2, a3, w_ref, b_ref, out_ref, acts):
    q = pos[2]
    for r, part in enumerate((a0, a1, a2, a3)):
        acts[pl.ds(pl.multiple_of((q ^ r) * 32, 32), 32), :] = part[...]
    pre = jnp.dot(acts[...], w_ref[...], preferred_element_type=F32)
    bias = b_ref[:, pl.ds(pl.multiple_of(q * 256, 256), 256)]
    codes = jnp.maximum(pre + bias, 0.0).astype(BF)
    for k in range(8):
        out_ref[k] = codes


def encode(pos, a0, a1, a2, a3, w, b):
    return call(
        encode_kernel,
        [SMEM] + [VMEM] * 6,
        [in_vmem((8, 128, 256), BF)],
        [pltpu.VMEM((128, 2048), BF)],
        2 * 128 * 2048 * 256,
        2 << 20,
    )(pos, a0, a1, a2, a3, w, b)[0]


def project_kernel(first, count, pos, own, other, w_hbm, out_ref, *rest):
    codes, slabs, sems = rest[-3:]
    layer, c = pos[0], pos[1]
    x, z = layer // NZ, layer % NZ

    def fetch(k):
        target = lax.rem(z + k + first, NZ)
        return pltpu.make_async_copy(w_hbm.at[:, target], slabs.at[k], sems.at[k])

    def start(k, _):
        fetch(k).start()
        return 0

    lax.fori_loop(0, count, start, 0)
    for xh in range(2):
        codes[:, pl.ds(pl.multiple_of((xh * 2 + c) * 256, 256), 256)] = own[xh]
        codes[:, pl.ds(pl.multiple_of((xh * 2 + 1 - c) * 256, 256), 256)] = other[xh]

    def advance(k, _):
        target = lax.rem(z + k + first, NZ)
        live = NZ + target >= layer
        fetch(k).wait()

        @pl.when(live)
        def _():
            w = jnp.concatenate([slabs[k, 0], slabs[k, 1]], axis=1)
            prod = jnp.dot(codes[...], w, preferred_element_type=F32)
            out_ref[k, x] = jnp.where(target >= layer, prod[:, :128], 0.0).astype(out_ref.dtype)
            out_ref[k, 1 - x] = prod[:, 128:].astype(out_ref.dtype)

        @pl.when(jnp.logical_not(live))
        def _():
            out_ref[k] = jnp.zeros((2, 512, 128), out_ref.dtype)

        return 0

    lax.fori_loop(0, count, advance, 0)
    if len(rest) > 3:
        rest[0][...] = codes[...].T


def project(pos, own, other, w, first, count, dtype, transposed):
    outs = [in_vmem((count, 2, 512, 128), dtype)]
    if transposed:
        outs.append(in_vmem((1024, 512), BF))
    return call(
        functools.partial(project_kernel, first, count),
        [SMEM, VMEM, VMEM, HBM],
        outs,
        [
            pltpu.VMEM((512, 1024), BF),
            pltpu.VMEM((count, 2, 1024, 128), BF),
            pltpu.SemaphoreType.DMA((count,)),
        ],
        count * 2 * 512 * 1024 * 256,
        count << 20,
    )(pos, own, other, w)


def backprop_kernel(dists, first_call, pos, *refs):
    count = len(refs) - (9 if first_call else 11)
    errs = refs[:count]
    codes_t, w_hbm = refs[count], refs[count + 1]
    dec_hbm, acc_ref, err, slabs, grads, in_sems, out_sems = refs[-7:]
    layer = pos[0]
    x, z = layer // NZ, layer % NZ
    targets = [lax.rem(z + d, NZ) for d in dists]
    fetches = [
        pltpu.make_async_copy(w_hbm.at[:, t], slabs.at[k], in_sems.at[k])
        for k, t in enumerate(targets)
    ]
    stores = [
        pltpu.make_async_copy(grads.at[k], dec_hbm.at[:, t], out_sems.at[k])
        for k, t in enumerate(targets)
    ]
    for fetch in fetches:
        fetch.start()
    if first_call:
        acc_ref[...] = jnp.zeros_like(acc_ref)
    for k, target in enumerate(targets):
        live = NZ + target >= layer
        fetches[k].wait()

        @pl.when(live)
        def _(k=k, target=target):
            zero = jnp.zeros((512, 128), BF)
            if count > len(dists):
                blocks = errs[0][...], errs[1][...]
                err[:, :128] = jnp.where(target >= layer, jnp.where(x == 0, *blocks), zero)
                err[:, 128:] = jnp.where(x == 0, *blocks[::-1])
            else:
                err[:, :128] = jnp.where(target >= layer, errs[k][x], zero)
                err[:, 128:] = errs[k][1 - x]
            e = err[...]
            grad = jnp.dot(codes_t[...], e, preferred_element_type=F32)
            grads[k, 0] = grad[:, :128].astype(BF)
            grads[k, 1] = grad[:, 128:].astype(BF)
            w = jnp.concatenate([slabs[k, 0], slabs[k, 1]], axis=1)
            acc_ref[...] += lax.dot_general(
                e, w, (((1,), (1,)), ((), ())), preferred_element_type=F32
            )

        @pl.when(jnp.logical_not(live))
        def _(k=k):
            grads[k] = jnp.zeros((2, 1024, 128), BF)

        stores[k].start()
    for store in stores:
        store.wait()


def backprop(pos, errs, dists, codes_t, w, carry=None):
    n, count = len(dists), len(errs)
    specs = [SMEM] + [VMEM] * count + [VMEM, HBM]
    args = [pos, *errs, codes_t, w]
    aliases = {}
    if carry is not None:
        specs += [HBM, VMEM]
        args += list(carry)
        aliases = {count + 3: 0, count + 4: 1}
    return call(
        functools.partial(backprop_kernel, dists, carry is None),
        specs,
        [in_hbm((2, NZ, 1024, 128), BF), in_vmem((512, 1024), F32)],
        [
            pltpu.VMEM((512, 256), BF),
            pltpu.VMEM((n, 2, 1024, 128), BF),
            pltpu.VMEM((n, 2, 1024, 128), BF),
            pltpu.SemaphoreType.DMA((n,)),
            pltpu.SemaphoreType.DMA((n,)),
        ],
        n * 4 * 512 * 1024 * 256,
        n << 20,
        aliases,
    )(*args)


def body(acts, w_enc, b_enc, w_dec, targets):
    layer = lax.axis_index("layer")
    tok = lax.axis_index("tok")
    pos = jnp.stack([layer, tok % 2, tok % 4]).astype(jnp.int32)

    a0 = acts[0]
    a1 = permute(a0, CORE_SWAP)
    a2 = permute(a0, XHI_SWAP)
    a3 = permute(a2, CORE_SWAP)
    w_full = swap_blocks(columns(w_enc[0]), None).reshape(2048, 256)
    block = encode(pos, a0, a1, a2, a3, w_full, b_enc)
    own = swap_blocks(block, G_CHIP).reshape(2, 512, 256)
    other = permute(own, CORE_SWAP)

    w = pltpu.with_memory_space_constraint(w_dec[0].reshape(2, NZ, 1024, 128), pltpu.HBM)
    (far,) = project(pos, own, other, w, 4, 1, BF, False)
    near, codes_t = project(pos, own, other, w, 5, 7, F32, True)
    parts = {d: near[d - 5] for d in (5, 6, 7)}
    parts.update({d: near[d + 3] for d in (0, 1, 2, 3)})
    up = permute(far[0, 0], Z_UP).astype(F32)
    down = permute(far[0, 1], Z_DOWN).astype(F32)
    up = jnp.stack([parts[3][0] + up, parts[3][1]])
    down = jnp.stack([parts[5][0], parts[5][1] + down])
    for hop in (2, 1, 0):
        up = permute(up.astype(BF), Z_UP).astype(F32)
        down = permute(down.astype(BF), Z_DOWN).astype(F32)
        if hop:
            up = up + parts[hop]
            down = down + parts[NZ - hop]
    total = parts[0] + up + down
    cross = permute(total[1].astype(BF), X_SWAP).astype(F32)
    err = (total[0] + cross - targets[0].astype(F32)).astype(BF)

    pair = jnp.stack([err, permute(err, X_SWAP)])
    ups, downs = [pair], [pair]
    for _ in range(1, 4):
        ups.append(permute(ups[-1], Z_UP))
        downs.append(permute(downs[-1], Z_DOWN))
    far_same = permute(ups[-1][0], Z_UP)
    far_other = permute(downs[-1][1], Z_DOWN)
    carry = backprop(pos, [pair], (0,), codes_t, w)
    for hop in (1, 2, 3):
        carry = backprop(pos, [ups[hop], downs[hop]], (NZ - hop, hop), codes_t, w, carry)
    dec_grad, partial = backprop(pos, [far_same, far_other], (4,), codes_t, w, carry)

    halves = partial.reshape(8, 2, 32, 1024)
    core = tok % 2
    keep = lax.dynamic_index_in_dim(halves, core, 1, keepdims=False)
    give = lax.dynamic_index_in_dim(halves, 1 - core, 1, keepdims=False)
    chip = keep + permute(give, CORE_SWAP)
    shares = swap_blocks(chip.astype(BF), G_OUT).astype(F32)
    code_grad = jnp.sum(shares, axis=0)
    return code_grad[None], dec_grad.reshape(1, NL, 1024, 128)


def solution(mesh):
    return jax.shard_map(
        body,
        mesh=mesh,
        in_specs=(
            P("layer", "tok", None),
            P("layer", "tok", None),
            P("layer", None),
            P("layer", None, None, "tok"),
            P("layer", None, "tok"),
        ),
        out_specs=(P("layer", "tok", None), P("layer", None, None, "tok")),
        check_vma=False,
    )
```

time: 167 us -> 170 us (1.018)
  the two profiles are of different devices: /device:TPU:32 before, /device:TPU:1 now
where the time goes in v2:
time: 170 us
  waiting for transfers between devices  56.6 us (33%)
  starting transfers between devices  48.6 us (29%)
  Pallas kernels  28.9 us (17%)
  blocking collectives  27.2 us (16%)
  local copies, waits for them, and re-layouts  4.32 us (3%)
  other arithmetic  3.05 us (2%)
    ppermute x23, waiting for transfers between devices, permute(): return lax.ppermute(x, AXES, pairs)  56.6 us
    ppermute x23, starting transfers between devices, permute(): return lax.ppermute(x, AXES, pairs)  40.2 us
    all_to_all x2, blocking collectives, swap_blocks(): return lax.all_to_all(x, 'tok', 0, 0, axis_index_groups=groups)  27.2 us
    pallas_call x5, Pallas kernels, backprop(): call(functools.partial(backprop_kernel, dists, carry is None), specs, [in...  19.5 us
    all_to_all x1, starting transfers between devices, swap_blocks(): return lax.all_to_all(x, 'tok', 0, 0, axis_index_groups=groups)  8.44 us
    pallas_call x2, Pallas kernels, project(): call(functools.partial(project_kernel, first, count), [SMEM, VMEM, VMEM,...  7.43 us
  transfers between devices with their start and end apart: 24, of which 14 were waited for; matrix products, arithmetic and copies ran while one was open for 1% of the time, Pallas kernels for 13%

profile of v2, /device:TPU:1, one launch (start us, length us, event | category | flops | bytes accessed | tf_op | source)
XLA Modules:
  0.0 169.5 jit_solution(4750887232834415749)
XLA Ops:
  0.6 0.9 copy-done
  1.6 1.0 shard_map.68
  2.6 8.4 %all-to-all-start = ((bf16[16,128,256]{2,1,0:T(8,128)(2,1)}), bf16[16,128,256]{2,1,0:T(8,128)(2,1)S(1)}, u32[]{:S(2)}, u32[]{:S(2)}) async-start(bf16[16,128,256]{2,1,0:T(8,128)(2,1)} %shard_map.68), calls=%async_computation | async-start | bytes 2097152 | tf_op jit(solution)/shard_map/all_to_all | solution.py:40
  11.1 2.9 %collective-permute-start.1 = (bf16[32,2048]{1,0:T(8,128)(2,1)}, bf16[32,2048]{1,0:T(8,128)(2,1)S(1)}, u32[]{:S(2)}, u32[]{:S(2)}) collective-permute-start(bf16[32,2048]{1,0:T(8,128)(2,1)} %bitcast.87), channel_id=1, source_target_pairs={{0,2},{1,3},{2,0},{3,1},{4,6},{5,7},{6,4},{7,5},{8,10},{9,11},{10,... | collective-permute-start | bytes 393224 | tf_op jit(solution)/shard_map/ppermute | solution.py:36
  13.9 0.7 collective-permute-start
  14.6 14.2 %collective-permute-done.1.a2 = bf16[32,2048]{1,0:T(8,128)(2,1)S(1)} collective-permute-done((bf16[32,2048]{1,0:T(8,128)(2,1)}, bf16[32,2048]{1,0:T(8,128)(2,1)S(1)}, u32[]{:S(2)}, u32[]{:S(2)}) %collective-permute-start.1) | collective-permute-done | bytes 131104 | tf_op jit(solution)/shard_map/ppermute | solution.py:36
  28.8 1.0 collective-permute-start.2
  29.8 0.1 pad_add_fusion.pos
  29.9 0.9 collective-permute-done.2.a3
  30.8 0.9 copy-done.3
  31.7 0.7 copy-done.4
  32.4 0.9 shard_map.69
  33.3 13.9 %all_to_all.15 = bf16[8,128,256]{2,1,0:T(8,128)(2,1)S(1)} all-to-all(bf16[8,128,256]{2,1,0:T(8,128)(2,1)S(1)} %shard_map.69), channel_id=1, replica_groups={{0,4,8,12,2,6,10,14},{1,5,9,13,3,7,11,15},{16,20,24,28,18,22,26,30},{17..., dimensions={0} | all-to-all | bytes 1048576 | tf_op jit(solution)/shard_map/all_to_all | solution.py:40
  47.2 2.4 %collective-permute-start.3 = (bf16[2,512,256]{2,1,0:T(8,128)(2,1)S(1)}, bf16[2,512,256]{2,1,0:T(8,128)(2,1)S(1)}, u32[]{:S(2)}, u32[]{:S(2)}) collective-permute-start(bf16[2,512,256]{2,1,0:T(8,128)(2,1)S(1)} %bitcast.83), channel_id=1, source_target_pairs={{0,1},{1,0},{2,3},{3,2},{4,5},{5,4},{6,7},{7,6},{8,9},{9,8},{10,11... | collective-permute-start | bytes 1572872 | tf_op jit(solution)/shard_map/ppermute | solution.py:36
  49.6 1.5 collective-permute-done.3.other
  51.1 2.2 %shard_map.71 = bf16[1,2,512,128]{3,2,1,0:T(8,128)(2,1)S(1)} custom-call(s32[3]{0:T(128)S(1)} %pad_add_fusion.pos, bf16[2,512,256]{2,1,0:T(8,128)(2,1)S(1)} %bitcast.84, bf16[2,512,256]{2,1,0:T(8,128)(2,1)S(1)} %collective-permute-done.3.other, bf16[2,8,1024,128]{3,2,1,0:T(8,128)(2,1)} %bitcast.90), custom_call_target="tpu_custom_call" | custom-call | flops 268435456 | bytes 1048576 | tf_op jit(solution)/shard_map/pallas_call | solution.py:146
  53.3 1.7 %collective-permute-start.4 = (bf16[512,128]{1,0:T(8,128)(2,1)S(1)}, bf16[512,128]{1,0:T(8,128)(2,1)S(1)}, u32[]{:S(2)}, u32[]{:S(2)}) collective-permute-start(bf16[512,128]{1,0:T(8,128)(2,1)S(1)} %get-tuple-element.34), channel_id=1, source_target_pairs={{0,16},{1,17},{2,18},{3,19},{4,20},{5,21},{6,22},{7,23},{8,24},{9,... | collective-permute-start | bytes 393224 | tf_op jit(solution)/shard_map/ppermute | solution.py:36
  55.0 4.0 %collective-permute-start.8 = (bf16[512,128]{1,0:T(8,128)(2,1)S(1)}, bf16[512,128]{1,0:T(8,128)(2,1)S(1)}, u32[]{:S(2)}, u32[]{:S(2)}) collective-permute-start(bf16[512,128]{1,0:T(8,128)(2,1)S(1)} %get-tuple-element.35), channel_id=1, source_target_pairs={{0,112},{1,113},{2,114},{3,115},{4,116},{5,117},{6,118},{7,119},{8... | collective-permute-start | bytes 393224 | tf_op jit(solution)/shard_map/ppermute | solution.py:36
  59.1 5.3 %shard_map.70 = (f32[7,2,512,128]{3,2,1,0:T(8,128)S(1)}, bf16[1024,512]{1,0:T(8,128)(2,1)S(1)}) custom-call(s32[3]{0:T(128)S(1)} %pad_add_fusion.pos, bf16[2,512,256]{2,1,0:T(8,128)(2,1)S(1)} %bitcast.85, bf16[2,512,256]{2,1,0:T(8,128)(2,1)S(1)} %collective-permute-done.3.other, bf16[2,8,1024,128]{3,2,1,0:T(8,128)(2,1)} %bitcast.91), custom_call_target="tpu_custom_call" | custom-call | flops 1879048192 | bytes 7340032 | tf_op jit(solution)/shard_map/pallas_call | solution.py:146
  64.3 0.3 convert.21
  64.7 0.0 collective-permute-done.4
  64.7 0.1 fusion.11
  64.8 0.0 copy-start.5
  64.9 1.5 collective-permute-start.9
  66.3 0.2 collective-permute-start.5
  66.5 5.6 %collective-permute-done.9 = bf16[2,512,128]{2,1,0:T(8,128)(2,1)S(1)} collective-permute-done((bf16[2,512,128]{2,1,0:T(8,128)(2,1)S(1)}, bf16[2,512,128]{2,1,0:T(8,128)(2,1)S(1)}, u32[]{:S(2)}, u32[]{:S(2)}) %collective-permute-start.9) | collective-permute-done | bytes 262176 | tf_op jit(solution)/shard_map/ppermute | solution.py:36
  72.1 2.1 %collective-permute-done.5 = bf16[2,512,128]{2,1,0:T(8,128)(2,1)S(1)} collective-permute-done((bf16[2,512,128]{2,1,0:T(8,128)(2,1)S(1)}, bf16[2,512,128]{2,1,0:T(8,128)(2,1)S(1)}, u32[]{:S(2)}, u32[]{:S(2)}) %collective-permute-start.5) | collective-permute-done | bytes 262176 | tf_op jit(solution)/shard_map/ppermute | solution.py:36
  74.3 0.1 fusion.4
  74.4 0.3 collective-permute-start.10
  74.7 1.3 collective-permute-start.6
  76.0 4.3 %collective-permute-done.10 = bf16[2,512,128]{2,1,0:T(8,128)(2,1)S(1)} collective-permute-done((bf16[2,512,128]{2,1,0:T(8,128)(2,1)S(1)}, bf16[2,512,128]{2,1,0:T(8,128)(2,1)S(1)}, u32[]{:S(2)}, u32[]{:S(2)}) %collective-permute-start.10) | collective-permute-done | bytes 262176 | tf_op jit(solution)/shard_map/ppermute | solution.py:36
  80.3 1.4 collective-permute-done.6
  81.7 0.1 fusion.3
  81.8 0.4 collective-permute-start.11
  82.2 1.2 collective-permute-start.7
  83.4 3.8 %collective-permute-done.11 = bf16[2,512,128]{2,1,0:T(8,128)(2,1)S(1)} collective-permute-done((bf16[2,512,128]{2,1,0:T(8,128)(2,1)S(1)}, bf16[2,512,128]{2,1,0:T(8,128)(2,1)S(1)}, u32[]{:S(2)}, u32[]{:S(2)}) %collective-permute-start.11) | collective-permute-done | bytes 262176 | tf_op jit(solution)/shard_map/ppermute | solution.py:36
  87.1 1.5 collective-permute-done.7
  88.6 0.1 fusion.5
  88.7 0.1 collective-permute-start.12
  88.8 3.8 %collective-permute-done.12 = bf16[512,128]{1,0:T(8,128)(2,1)S(1)} collective-permute-done((bf16[512,128]{1,0:T(8,128)(2,1)S(1)}, bf16[512,128]{1,0:T(8,128)(2,1)S(1)}, u32[]{:S(2)}, u32[]{:S(2)}) %collective-permute-start.12) | collective-permute-done | bytes 131104 | tf_op jit(solution)/shard_map/ppermute | solution.py:36
  92.6 0.1 fusion.8
  92.7 0.3 collective-permute-start.13
  93.0 5.1 %collective-permute-done.13 = bf16[512,128]{1,0:T(8,128)(2,1)S(1)} collective-permute-done((bf16[512,128]{1,0:T(8,128)(2,1)S(1)}, bf16[512,128]{1,0:T(8,128)(2,1)S(1)}, u32[]{:S(2)}, u32[]{:S(2)}) %collective-permute-start.13) | collective-permute-done | bytes 131104 | tf_op jit(solution)/shard_map/ppermute | solution.py:36
  98.1 0.4 collective-permute-start.14
  98.5 2.4 %collective-permute-start.18 = (bf16[2,512,128]{2,1,0:T(8,128)(2,1)S(1)}, bf16[2,512,128]{2,1,0:T(8,128)(2,1)}, u32[]{:S(2)}, u32[]{:S(2)}) collective-permute-start(bf16[2,512,128]{2,1,0:T(8,128)(2,1)S(1)} %pad_maximum_fusion.2.refs_0_), channel_id=1, source_target_pairs={{0,112},{1,113},{2,114},{3,115},{4,116},{5,117},{6,118},{7,119},{8... | collective-permute-start | bytes 786440 | tf_op jit(solution)/shard_map/ppermute | solution.py:36
  100.9 3.8 %collective-permute-done.14.refs_0_ = bf16[2,512,128]{2,1,0:T(8,128)(2,1)S(1)} collective-permute-done((bf16[2,512,128]{2,1,0:T(8,128)(2,1)S(1)}, bf16[2,512,128]{2,1,0:T(8,128)(2,1)S(1)}, u32[]{:S(2)}, u32[]{:S(2)}) %collective-permute-start.14) | collective-permute-done | bytes 262176 | tf_op jit(solution)/shard_map/ppermute | solution.py:36
  104.6 0.7 copy-done.1
  105.3 2.7 %collective-permute-start.19 = (bf16[2,512,128]{2,1,0:T(8,128)(2,1)}, bf16[2,512,128]{2,1,0:T(8,128)(2,1)}, u32[]{:S(2)}, u32[]{:S(2)}) collective-permute-start(bf16[2,512,128]{2,1,0:T(8,128)(2,1)} %collective-permute-done.18.refs_1_), channel_id=1, source_target_pairs={{0,112},{1,113},{2,114},{3,115},{4,116},{5,117},{6,118},{7,119},{8... | collective-permute-start | bytes 786440 | tf_op jit(solution)/shard_map/ppermute | solution.py:36
  108.0 6.1 %collective-permute-done.15.refs_0_ = bf16[2,512,128]{2,1,0:T(8,128)(2,1)} collective-permute-done((bf16[2,512,128]{2,1,0:T(8,128)(2,1)S(1)}, bf16[2,512,128]{2,1,0:T(8,128)(2,1)}, u32[]{:S(2)}, u32[]{:S(2)}) %collective-permute-start.15) | collective-permute-done | bytes 262176 | tf_op jit(solution)/shard_map/ppermute | solution.py:36
  114.1 3.3 %shard_map.72 = (bf16[2,8,1024,128]{3,2,1,0:T(8,128)(2,1)}, f32[512,1024]{1,0:T(8,128)S(1)}) custom-call(s32[3]{0:T(128)S(1)} %pad_add_fusion.pos, bf16[2,512,128]{2,1,0:T(8,128)(2,1)S(1)} %pad_maximum_fusion.2.refs_0_, bf16[1024,512]{1,0:T(8,128)(2,1)S(1)} %get-tuple-element.15.refs_1_.refs_2_, bf16[2,8,1024,128]{3,2,1,0:T(8,128)(2,1)} %bitcast.92), custom_call_target="tpu_custom_call" | custom-call | flops 536870912 | bytes 1048576 | tf_op jit(solution)/shard_map/pallas_call | solution.py:221
  117.4 2.7 %collective-permute-start.20 = (bf16[2,512,128]{2,1,0:T(8,128)(2,1)}, bf16[2,512,128]{2,1,0:T(8,128)(2,1)S(1)}, u32[]{:S(2)}, u32[]{:S(2)}) collective-permute-start(bf16[2,512,128]{2,1,0:T(8,128)(2,1)} %collective-permute-done.19.refs_1_), channel_id=1, source_target_pairs={{0,112},{1,113},{2,114},{3,115},{4,116},{5,117},{6,118},{7,119},{8... | collective-permute-start | bytes 786440 | tf_op jit(solution)/shard_map/ppermute | solution.py:36
  120.1 4.3 %shard_map.73 = (bf16[2,8,1024,128]{3,2,1,0:T(8,128)(2,1)}, f32[512,1024]{1,0:T(8,128)S(1)}) custom-call(s32[3]{0:T(128)S(1)} %pad_add_fusion.pos, bf16[2,512,128]{2,1,0:T(8,128)(2,1)S(1)} %copy-done.2, bf16[2,512,128]{2,1,0:T(8,128)(2,1)} %collective-permute-done.18.refs_1_, ...), custom_call_target="tpu_custom_call", output_to_operand_aliasing={{0}: (5, {}), {1}: (6, {})} | custom-call | flops 1073741824 | bytes 2097152 | tf_op jit(solution)/shard_map/pallas_call | solution.py:221
  124.5 0.9 slice_bitcast_fusion.2
  125.4 0.1 collective-permute-start.17
  125.5 2.7 %collective-permute-start.21 = (bf16[512,128]{1,0:T(8,128)(2,1)S(1)}, bf16[512,128]{1,0:T(8,128)(2,1)S(1)}, u32[]{:S(2)}, u32[]{:S(2)}) collective-permute-start(bf16[512,128]{1,0:T(8,128)(2,1)S(1)} %slice_bitcast_fusion.1), channel_id=1, source_target_pairs={{0,112},{1,113},{2,114},{3,115},{4,116},{5,117},{6,118},{7,119},{8... | collective-permute-start | bytes 393224 | tf_op jit(solution)/shard_map/ppermute | solution.py:36
  128.2 4.4 %shard_map.74 = (bf16[2,8,1024,128]{3,2,1,0:T(8,128)(2,1)}, f32[512,1024]{1,0:T(8,128)S(1)}) custom-call(s32[3]{0:T(128)S(1)} %pad_add_fusion.pos, bf16[2,512,128]{2,1,0:T(8,128)(2,1)} %collective-permute-done.15.refs_0_, bf16[2,512,128]{2,1,0:T(8,128)(2,1)} %collective-permute-done.19.refs_1_, ...), custom_call_target="tpu_custom_call", output_to_operand_aliasing={{0}: (5, {}), {1}: (6, {})} | custom-call | flops 1073741824 | bytes 2097152 | tf_op jit(solution)/shard_map/pallas_call | solution.py:221
  132.7 4.3 %shard_map.75 = (bf16[2,8,1024,128]{3,2,1,0:T(8,128)(2,1)}, f32[512,1024]{1,0:T(8,128)S(1)}) custom-call(s32[3]{0:T(128)S(1)} %pad_add_fusion.pos, bf16[2,512,128]{2,1,0:T(8,128)(2,1)} %collective-permute-done.16.refs_0_, bf16[2,512,128]{2,1,0:T(8,128)(2,1)S(1)} %collective-permute-done.20.refs_1_, ...), custom_call_target="tpu_custom_call", output_to_operand_aliasing={{0}: (5, {}), {1}: (6, {})} | custom-call | flops 1073741824 | bytes 2097152 | tf_op jit(solution)/shard_map/pallas_call | solution.py:221
  137.0 3.2 %shard_map.76 = (bf16[2,8,1024,128]{3,2,1,0:T(8,128)(2,1)}, f32[512,1024]{1,0:T(8,128)S(1)}) custom-call(s32[3]{0:T(128)S(1)} %pad_add_fusion.pos, bf16[512,128]{1,0:T(8,128)(2,1)S(1)} %collective-permute-done.17.refs_0_, bf16[512,128]{1,0:T(8,128)(2,1)S(1)} %collective-permute-done.21.refs_1_, ...), custom_call_target="tpu_custom_call", output_to_operand_aliasing={{0}: (5, {}), {1}: (6, {})} | custom-call | flops 536870912 | bytes 1048576 | tf_op jit(solution)/shard_map/pallas_call | solution.py:221
  140.2 0.1 dynamic-slice_bitcast_fusion
  140.3 11.5 %collective-permute-start.22 = (f32[8,32,1024]{2,1,0:T(8,128)S(1)}, f32[8,32,1024]{2,1,0:T(8,128)}, u32[]{:S(2)}, u32[]{:S(2)}) collective-permute-start(f32[8,32,1024]{2,1,0:T(8,128)S(1)} %dynamic-slice_bitcast_fusion), channel_id=1, source_target_pairs={{0,1},{1,0},{2,3},{3,2},{4,5},{5,4},{6,7},{7,6},{8,9},{9,8},{10,11... | collective-permute-start | bytes 3145736 | tf_op jit(solution)/shard_map/ppermute | solution.py:36
  151.8 2.4 %collective-permute-done.22 = f32[8,32,1024]{2,1,0:T(8,128)} collective-permute-done((f32[8,32,1024]{2,1,0:T(8,128)S(1)}, f32[8,32,1024]{2,1,0:T(8,128)}, u32[]{:S(2)}, u32[]{:S(2)}) %collective-permute-start.22) | collective-permute-done | bytes 1048608 | tf_op jit(solution)/shard_map/ppermute | solution.py:36
  154.2 1.4 fusion
  155.5 13.3 %all_to_all.16 = bf16[8,32,1024]{2,1,0:T(8,128)(2,1)S(1)} all-to-all(bf16[8,32,1024]{2,1,0:T(8,128)(2,1)S(1)} %fusion), channel_id=1, replica_groups={{0,2,4,6,8,10,12,14},{1,3,5,7,9,11,13,15},{16,18,20,22,24,26,28,30},{17..., dimensions={0} | all-to-all | bytes 1048576 | tf_op jit(solution)/shard_map/all_to_all | solution.py:40
  168.8 0.7 convert_reduce_fusion
  (25 shorter events, 0.2 us)
Async XLA Ops:
  0.6 1.0 copy-start
  2.6 28.2 %all-to-all-start = ((bf16[16,128,256]{2,1,0:T(8,128)(2,1)}), bf16[16,128,256]{2,1,0:T(8,128)(2,1)S(1)}, u32[]{:S(2)}, u32[]{:S(2)}) async-start(bf16[16,128,256]{2,1,0:T(8,128)(2,1)} %shard_map.68), calls=%async_computation | async-start | bytes 2097152 | tf_op jit(solution)/shard_map/all_to_all | solution.py:40
  11.1 17.8 %collective-permute-start.1 = (bf16[32,2048]{1,0:T(8,128)(2,1)}, bf16[32,2048]{1,0:T(8,128)(2,1)S(1)}, u32[]{:S(2)}, u32[]{:S(2)}) collective-permute-start(bf16[32,2048]{1,0:T(8,128)(2,1)} %bitcast.87), channel_id=1, source_target_pairs={{0,2},{1,3},{2,0},{3,1},{4,6},{5,7},{6,4},{7,5},{8,10},{9,11},{10,... | collective-permute-start | bytes 393224 | tf_op jit(solution)/shard_map/ppermute | solution.py:36
  13.9 16.0 %collective-permute-start = (bf16[32,2048]{1,0:T(8,128)(2,1)}, bf16[32,2048]{1,0:T(8,128)(2,1)S(1)}, u32[]{:S(2)}, u32[]{:S(2)}) collective-permute-start(bf16[32,2048]{1,0:T(8,128)(2,1)} %bitcast.88), channel_id=1, source_target_pairs={{0,1},{1,0},{2,3},{3,2},{4,5},{5,4},{6,7},{7,6},{8,9},{9,8},{10,11... | collective-permute-start | bytes 393224 | tf_op jit(solution)/shard_map/ppermute | solution.py:36
  28.8 2.0 %collective-permute-start.2 = (bf16[32,2048]{1,0:T(8,128)(2,1)S(1)}, bf16[32,2048]{1,0:T(8,128)(2,1)S(1)}, u32[]{:S(2)}, u32[]{:S(2)}) collective-permute-start(bf16[32,2048]{1,0:T(8,128)(2,1)S(1)} %collective-permute-done.1.a2), channel_id=1, source_target_pairs={{0,1},{1,0},{2,3},{3,2},{4,5},{5,4},{6,7},{7,6},{8,9},{9,8},{10,11... | collective-permute-start | bytes 393224 | tf_op jit(solution)/shard_map/ppermute | solution.py:36
  30.8 0.9 copy-start.3
  31.7 0.7 copy-start.4
  47.2 4.0 %collective-permute-start.3 = (bf16[2,512,256]{2,1,0:T(8,128)(2,1)S(1)}, bf16[2,512,256]{2,1,0:T(8,128)(2,1)S(1)}, u32[]{:S(2)}, u32[]{:S(2)}) collective-permute-start(bf16[2,512,256]{2,1,0:T(8,128)(2,1)S(1)} %bitcast.83), channel_id=1, source_target_pairs={{0,1},{1,0},{2,3},{3,2},{4,5},{5,4},{6,7},{7,6},{8,9},{9,8},{10,11... | collective-permute-start | bytes 1572872 | tf_op jit(solution)/shard_map/ppermute | solution.py:36
  53.3 11.4 %collective-permute-start.4 = (bf16[512,128]{1,0:T(8,128)(2,1)S(1)}, bf16[512,128]{1,0:T(8,128)(2,1)S(1)}, u32[]{:S(2)}, u32[]{:S(2)}) collective-permute-start(bf16[512,128]{1,0:T(8,128)(2,1)S(1)} %get-tuple-element.34), channel_id=1, source_target_pairs={{0,16},{1,17},{2,18},{3,19},{4,20},{5,21},{6,22},{7,23},{8,24},{9,... | collective-permute-start | bytes 393224 | tf_op jit(solution)/shard_map/ppermute | solution.py:36
  55.0 9.7 %collective-permute-start.8 = (bf16[512,128]{1,0:T(8,128)(2,1)S(1)}, bf16[512,128]{1,0:T(8,128)(2,1)S(1)}, u32[]{:S(2)}, u32[]{:S(2)}) collective-permute-start(bf16[512,128]{1,0:T(8,128)(2,1)S(1)} %get-tuple-element.35), channel_id=1, source_target_pairs={{0,112},{1,113},{2,114},{3,115},{4,116},{5,117},{6,118},{7,119},{8... | collective-permute-start | bytes 393224 | tf_op jit(solution)/shard_map/ppermute | solution.py:36
  64.8 27.8 %copy-start.5 = (bf16[1,512,128]{2,1,0:T(8,128)(2,1)S(1)}, bf16[1,512,128]{2,1,0:T(8,128)(2,1)}, u32[]{:S(2)}) copy-start(bf16[1,512,128]{2,1,0:T(8,128)(2,1)} %param.9) | copy-start | bytes 393220
  64.9 7.3 %collective-permute-start.9 = (bf16[2,512,128]{2,1,0:T(8,128)(2,1)S(1)}, bf16[2,512,128]{2,1,0:T(8,128)(2,1)S(1)}, u32[]{:S(2)}, u32[]{:S(2)}) collective-permute-start(bf16[2,512,128]{2,1,0:T(8,128)(2,1)S(1)} %pad_maximum_fusion.1), channel_id=1, source_target_pairs={{0,112},{1,113},{2,114},{3,115},{4,116},{5,117},{6,118},{7,119},{8... | collective-permute-start | bytes 786440 | tf_op jit(solution)/shard_map/ppermute | solution.py:36
  66.3 7.9 %collective-permute-start.5 = (bf16[2,512,128]{2,1,0:T(8,128)(2,1)S(1)}, bf16[2,512,128]{2,1,0:T(8,128)(2,1)S(1)}, u32[]{:S(2)}, u32[]{:S(2)}) collective-permute-start(bf16[2,512,128]{2,1,0:T(8,128)(2,1)S(1)} %pad_maximum_fusion), channel_id=1, source_target_pairs={{0,16},{1,17},{2,18},{3,19},{4,20},{5,21},{6,22},{7,23},{8,24},{9,... | collective-permute-start | bytes 786440 | tf_op jit(solution)/shard_map/ppermute | solution.py:36
  74.4 5.9 %collective-permute-start.10 = (bf16[2,512,128]{2,1,0:T(8,128)(2,1)S(1)}, bf16[2,512,128]{2,1,0:T(8,128)(2,1)S(1)}, u32[]{:S(2)}, u32[]{:S(2)}) collective-permute-start(bf16[2,512,128]{2,1,0:T(8,128)(2,1)S(1)} %get-tuple-element.29), channel_id=1, source_target_pairs={{0,112},{1,113},{2,114},{3,115},{4,116},{5,117},{6,118},{7,119},{8... | collective-permute-start | bytes 786440 | tf_op jit(solution)/shard_map/ppermute | solution.py:36
  74.7 7.0 %collective-permute-start.6 = (bf16[2,512,128]{2,1,0:T(8,128)(2,1)S(1)}, bf16[2,512,128]{2,1,0:T(8,128)(2,1)S(1)}, u32[]{:S(2)}, u32[]{:S(2)}) collective-permute-start(bf16[2,512,128]{2,1,0:T(8,128)(2,1)S(1)} %get-tuple-element.28), channel_id=1, source_target_pairs={{0,16},{1,17},{2,18},{3,19},{4,20},{5,21},{6,22},{7,23},{8,24},{9,... | collective-permute-start | bytes 786440 | tf_op jit(solution)/shard_map/ppermute | solution.py:36
  81.8 5.3 %collective-permute-start.11 = (bf16[2,512,128]{2,1,0:T(8,128)(2,1)S(1)}, bf16[2,512,128]{2,1,0:T(8,128)(2,1)S(1)}, u32[]{:S(2)}, u32[]{:S(2)}) collective-permute-start(bf16[2,512,128]{2,1,0:T(8,128)(2,1)S(1)} %get-tuple-element.27), channel_id=1, source_target_pairs={{0,112},{1,113},{2,114},{3,115},{4,116},{5,117},{6,118},{7,119},{8... | collective-permute-start | bytes 786440 | tf_op jit(solution)/shard_map/ppermute | solution.py:36
  82.2 6.4 %collective-permute-start.7 = (bf16[2,512,128]{2,1,0:T(8,128)(2,1)S(1)}, bf16[2,512,128]{2,1,0:T(8,128)(2,1)S(1)}, u32[]{:S(2)}, u32[]{:S(2)}) collective-permute-start(bf16[2,512,128]{2,1,0:T(8,128)(2,1)S(1)} %get-tuple-element.26), channel_id=1, source_target_pairs={{0,16},{1,17},{2,18},{3,19},{4,20},{5,21},{6,22},{7,23},{8,24},{9,... | collective-permute-start | bytes 786440 | tf_op jit(solution)/shard_map/ppermute | solution.py:36
  88.7 3.9 %collective-permute-start.12 = (bf16[512,128]{1,0:T(8,128)(2,1)S(1)}, bf16[512,128]{1,0:T(8,128)(2,1)S(1)}, u32[]{:S(2)}, u32[]{:S(2)}) collective-permute-start(bf16[512,128]{1,0:T(8,128)(2,1)S(1)} %fusion.13), channel_id=1, source_target_pairs={{0,128},{1,129},{2,130},{3,131},{4,132},{5,133},{6,134},{7,135},{8... | collective-permute-start | bytes 393224 | tf_op jit(solution)/shard_map/ppermute | solution.py:36
  92.7 5.4 %collective-permute-start.13 = (bf16[512,128]{1,0:T(8,128)(2,1)S(1)}, bf16[512,128]{1,0:T(8,128)(2,1)S(1)}, u32[]{:S(2)}, u32[]{:S(2)}) collective-permute-start(bf16[512,128]{1,0:T(8,128)(2,1)S(1)} %fusion.8), channel_id=1, source_target_pairs={{0,128},{1,129},{2,130},{3,131},{4,132},{5,133},{6,134},{7,135},{8... | collective-permute-start | bytes 393224 | tf_op jit(solution)/shard_map/ppermute | solution.py:36
  98.1 6.5 %collective-permute-start.14 = (bf16[2,512,128]{2,1,0:T(8,128)(2,1)S(1)}, bf16[2,512,128]{2,1,0:T(8,128)(2,1)S(1)}, u32[]{:S(2)}, u32[]{:S(2)}) collective-permute-start(bf16[2,512,128]{2,1,0:T(8,128)(2,1)S(1)} %pad_maximum_fusion.2.refs_0_), channel_id=1, source_target_pairs={{0,16},{1,17},{2,18},{3,19},{4,20},{5,21},{6,22},{7,23},{8,24},{9,... | collective-permute-start | bytes 786440 | tf_op jit(solution)/shard_map/ppermute | solution.py:36
  98.5 6.8 %collective-permute-start.18 = (bf16[2,512,128]{2,1,0:T(8,128)(2,1)S(1)}, bf16[2,512,128]{2,1,0:T(8,128)(2,1)}, u32[]{:S(2)}, u32[]{:S(2)}) collective-permute-start(bf16[2,512,128]{2,1,0:T(8,128)(2,1)S(1)} %pad_maximum_fusion.2.refs_0_), channel_id=1, source_target_pairs={{0,112},{1,113},{2,114},{3,115},{4,116},{5,117},{6,118},{7,119},{8... | collective-permute-start | bytes 786440 | tf_op jit(solution)/shard_map/ppermute | solution.py:36
  104.6 9.4 %collective-permute-start.15 = (bf16[2,512,128]{2,1,0:T(8,128)(2,1)S(1)}, bf16[2,512,128]{2,1,0:T(8,128)(2,1)}, u32[]{:S(2)}, u32[]{:S(2)}) collective-permute-start(bf16[2,512,128]{2,1,0:T(8,128)(2,1)S(1)} %collective-permute-done.14.refs_0_), channel_id=1, source_target_pairs={{0,16},{1,17},{2,18},{3,19},{4,20},{5,21},{6,22},{7,23},{8,24},{9,... | collective-permute-start | bytes 786440 | tf_op jit(solution)/shard_map/ppermute | solution.py:36
  104.6 0.7 copy-start.1
  105.3 12.0 %collective-permute-start.19 = (bf16[2,512,128]{2,1,0:T(8,128)(2,1)}, bf16[2,512,128]{2,1,0:T(8,128)(2,1)}, u32[]{:S(2)}, u32[]{:S(2)}) collective-permute-start(bf16[2,512,128]{2,1,0:T(8,128)(2,1)} %collective-permute-done.18.refs_1_), channel_id=1, source_target_pairs={{0,112},{1,113},{2,114},{3,115},{4,116},{5,117},{6,118},{7,119},{8... | collective-permute-start | bytes 786440 | tf_op jit(solution)/shard_map/ppermute | solution.py:36
  114.1 10.4 %collective-permute-start.16 = (bf16[2,512,128]{2,1,0:T(8,128)(2,1)}, bf16[2,512,128]{2,1,0:T(8,128)(2,1)}, u32[]{:S(2)}, u32[]{:S(2)}) collective-permute-start(bf16[2,512,128]{2,1,0:T(8,128)(2,1)} %collective-permute-done.15.refs_0_), channel_id=1, source_target_pairs={{0,16},{1,17},{2,18},{3,19},{4,20},{5,21},{6,22},{7,23},{8,24},{9,... | collective-permute-start | bytes 786440 | tf_op jit(solution)/shard_map/ppermute | solution.py:36
  114.1 6.0 %copy-start.2 = (bf16[2,512,128]{2,1,0:T(8,128)(2,1)S(1)}, bf16[2,512,128]{2,1,0:T(8,128)(2,1)}, u32[]{:S(2)}) copy-start(bf16[2,512,128]{2,1,0:T(8,128)(2,1)} %copy-done.1) | copy-start | bytes 786436
  117.4 8.1 %collective-permute-start.20 = (bf16[2,512,128]{2,1,0:T(8,128)(2,1)}, bf16[2,512,128]{2,1,0:T(8,128)(2,1)S(1)}, u32[]{:S(2)}, u32[]{:S(2)}) collective-permute-start(bf16[2,512,128]{2,1,0:T(8,128)(2,1)} %collective-permute-done.19.refs_1_), channel_id=1, source_target_pairs={{0,112},{1,113},{2,114},{3,115},{4,116},{5,117},{6,118},{7,119},{8... | collective-permute-start | bytes 786440 | tf_op jit(solution)/shard_map/ppermute | solution.py:36
  125.4 11.6 %collective-permute-start.17 = (bf16[512,128]{1,0:T(8,128)(2,1)S(1)}, bf16[512,128]{1,0:T(8,128)(2,1)S(1)}, u32[]{:S(2)}, u32[]{:S(2)}) collective-permute-start(bf16[512,128]{1,0:T(8,128)(2,1)S(1)} %slice_bitcast_fusion.2), channel_id=1, source_target_pairs={{0,16},{1,17},{2,18},{3,19},{4,20},{5,21},{6,22},{7,23},{8,24},{9,... | collective-permute-start | bytes 393224 | tf_op jit(solution)/shard_map/ppermute | solution.py:36
  125.5 11.5 %collective-permute-start.21 = (bf16[512,128]{1,0:T(8,128)(2,1)S(1)}, bf16[512,128]{1,0:T(8,128)(2,1)S(1)}, u32[]{:S(2)}, u32[]{:S(2)}) collective-permute-start(bf16[512,128]{1,0:T(8,128)(2,1)S(1)} %slice_bitcast_fusion.1), channel_id=1, source_target_pairs={{0,112},{1,113},{2,114},{3,115},{4,116},{5,117},{6,118},{7,119},{8... | collective-permute-start | bytes 393224 | tf_op jit(solution)/shard_map/ppermute | solution.py:36
  140.3 13.9 %collective-permute-start.22 = (f32[8,32,1024]{2,1,0:T(8,128)S(1)}, f32[8,32,1024]{2,1,0:T(8,128)}, u32[]{:S(2)}, u32[]{:S(2)}) collective-permute-start(f32[8,32,1024]{2,1,0:T(8,128)S(1)} %dynamic-slice_bitcast_fusion), channel_id=1, source_target_pairs={{0,1},{1,0},{2,3},{3,2},{4,5},{5,4},{6,7},{7,6},{8,9},{9,8},{10,11... | collective-permute-start | bytes 3145736 | tf_op jit(solution)/shard_map/ppermute | solution.py:36
